TPU v7x, 1024 devices: a whole 8x8x8 slice. The times are simulated.
1024 devices in a mesh: ctx: 128 (over z, y, core), head: 8 (over x).
Axes of the slice: x: 8, y: 8, z: 8, core: 2. Of those that a mesh axis runs over, the one named last changes fastest.
Arguments:
- queries: bfloat16 [16384, 4096], P('ctx', 'head'), may hold values from -3 to 3
- key_rows: bfloat16 [16384, 4096], P('ctx', 'head'), may hold values from -3 to 3
- value_rows: bfloat16 [16384, 4096], P('ctx', 'head'), may hold values from -6 to 6
- out_grad: bfloat16 [16384, 4096], P('ctx', 'head'), may hold values from -6 to 6
- log_decay: float32 [32, 16384], P('head', 'ctx'), as said below
- doc_start: int32 [16384], P('ctx'), may hold values from 0 to 8128, as said below
- norm_gain: float32 [4096], P('head'), may hold values from 0.5 to 1.5
Outputs:
- normed: bfloat16 [16384, 4096], P('ctx', 'head')
- query_grad: bfloat16 [16384, 4096], P('ctx', 'head')
- key_grad: bfloat16 [16384, 4096], P('ctx', 'head')
- value_grad: bfloat16 [16384, 4096], P('ctx', 'head')
Inputs may be any that keep to these rules, and one draw needn't show every extreme that they name: `log_decay`: every entry is negative. doc_start never falls along the batch and equals the token's own position at each document's first token; the first document starts at 0, and one document starts exactly at 8128 and runs to the end of the batch.
All inputs are finite; a program needn't handle non-finite values.
Results may differ from a plain program's by a relative error of at most 0.0055.
Values sent between devices are 32-bit elements; how exact they have to be, the bound alone decides.
No kernel may reach another device: no remote copies, remote signals or barrier semaphores. Data moves between devices by JAX's collectives and lax.ppermute only.
A program may use at most 128 MiB of HBM per device.

v0:
```python
import jax
import jax.numpy as jnp
from jax import lax
from jax.sharding import PartitionSpec as P

ATTN_GROUPS = 32
DH = 128


EPSILON = 1e-06


def prefix(array, axis, combine, identity, reverse):
    peers, position = (lax.axis_size(axis), lax.axis_index(axis))
    everything = jax.tree.map(lambda part: lax.all_gather(part, axis), array)
    start = jax.tree.map(
        lambda part, zero: jnp.broadcast_to(jnp.asarray(zero, part.dtype), part.shape),
        array,
        identity,
    )

    def turn(k, before):
        at = peers - 1 - k if reverse else k
        reached = at > position if reverse else at < position
        new = combine(before, jax.tree.map(lambda part: part[at], everything))
        return jax.tree.map(lambda a, b: jnp.where(reached, a, b), new, before)

    return lax.fori_loop(0, peers, turn, start)


def decay_tables(cum_decay, doc_rows, start):
    count = doc_rows.shape[0]
    places = jnp.arange(count)
    visible = (doc_rows[:, None] == doc_rows[None, :]) & (places[:, None] >= places[None, :])
    spread = cum_decay[:, :, None] - cum_decay[:, None, :]
    decay_mat = jnp.where(visible[None], jnp.exp(jnp.where(visible[None], spread, 0.0)), 0.0)
    continue_mask = (doc_rows < start).astype(jnp.float32)
    ending = (doc_rows == doc_rows[-1]).astype(jnp.float32)
    inward = jnp.exp(cum_decay) * continue_mask[None, :]
    outward = jnp.exp(cum_decay[:, -1:] - cum_decay) * ending[None, :]
    factor = jnp.exp(cum_decay[:, -1]) * (doc_rows[-1] < start).astype(jnp.float32)
    return (decay_mat, inward, outward, factor)


def combine(earlier, later):
    return (earlier[0] * later[0], later[0][:, None, None] * earlier[1] + later[1])


def on_device(queries, key_rows, value_rows, out_grad, log_decay, doc_start, norm_gain):
    rows = queries.shape[0]
    local_heads = queries.shape[1] // DH
    start = lax.axis_index("ctx") * rows
    query_h = queries.reshape(rows, local_heads, DH)
    key_h = key_rows.reshape(rows, local_heads, DH)
    value_h = value_rows.reshape(rows, local_heads, DH)
    cum_decay = jnp.cumsum(log_decay, axis=1)
    decay_mat, inward, outward, factor = decay_tables(cum_decay, doc_start, start)
    weighted = (key_h.astype(jnp.float32) * outward.T[:, :, None]).astype(jnp.bfloat16)
    local_state = jnp.einsum("thi,thj->hij", weighted, value_h, preferred_element_type=jnp.float32)
    identity = (jnp.ones_like(factor), jnp.zeros_like(local_state))
    incoming = prefix((factor, local_state), "ctx", combine, identity, False)[1]
    highest = lax.Precision.HIGHEST
    scores = (
        jnp.einsum("thd,shd->hts", query_h, key_h, preferred_element_type=jnp.float32) * decay_mat
    )
    attend = scores.astype(jnp.bfloat16)
    inner = jnp.einsum("hts,shd->thd", attend, value_h, preferred_element_type=jnp.float32)
    carried = jnp.einsum("thi,hij->thj", query_h.astype(jnp.float32), incoming, precision=highest)
    output = (inner + inward.T[:, :, None] * carried).reshape(rows, local_heads * DH)
    scaled_grad = out_grad.astype(jnp.float32) * norm_gain
    square_sum, cross_sum = lax.psum(
        (jnp.sum(output * output, axis=1), jnp.sum(scaled_grad * output, axis=1)), "head"
    )
    width = ATTN_GROUPS * DH
    inverse = lax.rsqrt(square_sum / width + EPSILON)
    cross = cross_sum / width
    normed = (output * inverse[:, None] * norm_gain).astype(jnp.bfloat16)
    grad_out = (inverse[:, None] * scaled_grad - output * (inverse**3 * cross)[:, None]).astype(
        jnp.bfloat16
    )
    grad_h = grad_out.reshape(rows, local_heads, DH)
    gated = (query_h.astype(jnp.float32) * inward.T[:, :, None]).astype(jnp.bfloat16)
    grad_state = jnp.einsum("thi,thj->hij", gated, grad_h, preferred_element_type=jnp.float32)
    outgoing = prefix((factor, grad_state), "ctx", combine, identity, True)[1]
    mixing = (
        jnp.einsum("thd,shd->hts", grad_h, value_h, preferred_element_type=jnp.float32) * decay_mat
    ).astype(jnp.bfloat16)
    query_grad = jnp.einsum(
        "hts,shd->thd", mixing, key_h, preferred_element_type=jnp.float32
    ) + inward.T[:, :, None] * jnp.einsum(
        "thj,hij->thi", grad_h.astype(jnp.float32), incoming, precision=highest
    )
    key_grad = jnp.einsum(
        "hts,thd->shd", mixing, query_h, preferred_element_type=jnp.float32
    ) + outward.T[:, :, None] * jnp.einsum(
        "shj,hij->shi", value_h.astype(jnp.float32), outgoing, precision=highest
    )
    value_grad = jnp.einsum(
        "hts,thd->shd", attend, grad_h, preferred_element_type=jnp.float32
    ) + outward.T[:, :, None] * jnp.einsum(
        "shi,hij->shj", key_h.astype(jnp.float32), outgoing, precision=highest
    )
    shape_out = (rows, local_heads * DH)
    return (
        normed,
        query_grad.reshape(shape_out).astype(jnp.bfloat16),
        key_grad.reshape(shape_out).astype(jnp.bfloat16),
        value_grad.reshape(shape_out).astype(jnp.bfloat16),
    )


def solution(mesh):
    placed = (
        P("ctx", "head"),
        P("ctx", "head"),
        P("ctx", "head"),
        P("ctx", "head"),
        P("head", "ctx"),
        P("ctx"),
        P("head"),
    )
    return jax.shard_map(
        on_device,
        mesh=mesh,
        in_specs=placed,
        out_specs=(P("ctx", "head"), P("ctx", "head"), P("ctx", "head"), P("ctx", "head")),
        check_vma=False,
    )
```

profile of v0, /device:TPU:1, one launch (start us, length us, event | category | flops | bytes accessed | tf_op | source)
XLA Modules:
  0.0 738.8 jit_solution(372011485791483276)
XLA Ops:
  7.2 1.2 slice.9
  9.1 1.3 compare_convert_fusion.1
  14.7 1.3 dynamic-slice
  16.9 265.9 %all-reduce = f32[512]{0:T(512)S(1)} all-reduce(f32[512]{0:T(512)S(1)} %dynamic-update-slice), channel_id=2, replica_groups=mesh['ctx'=128,'head'=8] {'ctx'}, use_global_device_ids=true, to_apply=%add | all-reduce | flops 512 | bytes 4096
  284.3 140.4 %while.30 = (s32[]{:T(128)}, f32[4,128,128]{2,1,0:T(8,128)S(1)}, s32[]{:T(128)}, f32[128,4]{1,0:T(8,128)S(1)}, f32[128,4,128,128]{3,2,1,0:T(8,128)}, /*index=5*/s32[]{:T(128)}, s32[]{:T(128)}) while((s32[]{:T(128)}, f32[4,128,128]{2,1,0:T(8,128)S(1)}, s32[]{:T(128)}, f32[128,4]{1,0:T(8,128)S(1)}, f32[128,4,128,128]{3,2,1,0:T(8,128)}, ...), condition=%wide.region_2.3_spmd.clone, body=%wide.region_1.2_spmd.clone.sunk | while | flops 262148 | bytes 786593 | solution.py:28
  426.3 13.5 %all-reduce.1 = (f32[128]{0:T(128)S(1)}, f32[128]{0:T(128)S(1)}) all-reduce(f32[128]{0:T(128)S(1)} %get-tuple-element.312, f32[128]{0:T(128)S(1)} %multiply_reduce_fusion), channel_id=1, replica_groups=mesh['ctx'=128,'head'=8] {'head'}, use_global_device_ids=true, to_apply=%region_4.5 | all-reduce | flops 256 | bytes 2048 | tf_op jit(solution)/shard_map/psum | solution.py:71
  439.8 1.7 subtract_convert_fusion
  444.4 143.7 %all-gather.8.cloned.1.call-done = f32[512,128,128]{2,1,0:T(8,128)} async-done(((f32[4,128,128]{2,1,0:T(8,128)}), f32[512,128,128]{2,1,0:T(8,128)}) %all-gather.8.cloned.1.call-update) | async-done | bytes 33554448 | tf_op jit(solution)/shard_map/all_gather | solution.py:15
  588.1 141.6 %while.31 = (s32[]{:T(128)}, f32[4,128,128]{2,1,0:T(8,128)S(1)}, s32[]{:T(128)}, f32[128,4]{1,0:T(8,128)S(1)}, f32[128,4,128,128]{3,2,1,0:T(8,128)}, /*index=5*/s32[]{:T(128)}, s32[]{:T(128)}, s32[]{:T(128)}, s32[]{:T(128)}) while((s32[]{:T(128)}, f32[4,128,128]{2,1,0:T(8,128)S(1)}, s32[]{:T(128)}, f32[128,4]{1,0:T(8,128)S(1)}, ...), condition=%wide.region_8.9_spmd.clone, body=%wide.region_7.8_spmd.clone.sunk | while | flops 262152 | bytes 786655 | solution.py:28
  589.2 1.1 fusion.54
  590.3 1.1 fusion.54
  591.4 1.1 fusion.54
  592.5 1.1 fusion.54
  593.6 1.1 fusion.54
  594.7 1.1 fusion.54
  595.8 1.1 fusion.54
  596.9 1.1 fusion.54
  598.1 1.1 fusion.54
  599.2 1.1 fusion.54
  600.3 1.1 fusion.54
  601.4 1.1 fusion.54
  602.5 1.1 fusion.54
  603.6 1.1 fusion.54
  604.7 1.1 fusion.54
  605.8 1.1 fusion.54
  606.9 1.1 fusion.54
  608.0 1.1 fusion.54
  609.1 1.1 fusion.54
  610.2 1.1 fusion.54
  611.3 1.1 fusion.54
  612.4 1.1 fusion.54
  613.5 1.1 fusion.54
  614.6 1.1 fusion.54
  615.8 1.1 fusion.54
  616.9 1.1 fusion.54
  618.0 1.1 fusion.54
  619.1 1.1 fusion.54
  620.2 1.1 fusion.54
  621.3 1.1 fusion.54
  622.4 1.1 fusion.54
  623.5 1.1 fusion.54
  624.6 1.1 fusion.54
  625.7 1.1 fusion.54
  626.8 1.1 fusion.54
  627.9 1.1 fusion.54
  629.0 1.1 fusion.54
  630.1 1.1 fusion.54
  631.2 1.1 fusion.54
  632.3 1.1 fusion.54
  633.5 1.1 fusion.54
  634.6 1.1 fusion.54
  641.2 1.1 fusion.54
  646.7 1.1 fusion.54
  652.3 1.1 fusion.54
  662.2 1.1 fusion.54
  667.8 1.1 fusion.54
  673.3 1.1 fusion.54
  683.2 1.1 fusion.54
  688.8 1.1 fusion.54
  694.3 1.1 fusion.54
  704.3 1.1 fusion.54
  709.8 1.1 fusion.54
  715.3 1.1 fusion.54
  725.3 1.1 fusion.54
  (494 shorter events, 227.0 us)
Async XLA Ops:
  7.2 5.5 copy-start
  7.2 277.1 %all-gather.6.cloned.1.call-start = ((), (), s32[]{:S(2)}) async-start(), calls=%async_computation | async-start | bytes 33816576 | tf_op jit(solution)/shard_map/all_gather | solution.py:15
  13.6 574.5 %all-gather.8.cloned.1.call-start = ((), (), s32[]{:S(2)}) async-start(), calls=%async_computation.1 | async-start | bytes 33816576 | tf_op jit(solution)/shard_map/all_gather | solution.py:15
Sparse Core Ops, SparseCore 0:
  13.7 161.9 all-gather.5
  442.7 145.3 all-gather.7
where the time goes:
time: 747 us; the launch traced here: 739 us
  blocking collectives  279 us (37%)
  other arithmetic  276 us (37%)
  waiting for transfers between devices  144 us (19%)
  between operations  15.5 us (2%)
  local copies, waits for them, and re-layouts  9.97 us (1%)
  loops' own time  9.66 us (1%)
    select_n x256, other arithmetic, turn(): return jax.tree.map(lambda a, b: jnp.where(reached, a, b), new, before)  270 us
    unnamed x1, blocking collectives  266 us
    all_gather x2, waiting for transfers between devices, prefix(): everything = jax.tree.map(lambda part: lax.all_gather(part, axis), array)  144 us
  transfers between devices with their start and end apart: 2, of which 1 were waited for; matrix products, arithmetic and copies ran while one was open for 1% of the time, Pallas kernels for 0%

commit v1 on v0

v1 whole, which is shorter than its diff:
```python
import jax
import jax.numpy as jnp
from jax import lax
from jax.experimental import pallas as pl
from jax.experimental.pallas import tpu as pltpu
from jax.sharding import PartitionSpec as P

ATTN_GROUPS = 32
DH = 128
EPSILON = 1e-06
HALF = 64
SUB = 8

F32 = jnp.float32
BF16 = jnp.bfloat16
HIGH = lax.Precision.HIGHEST
GROUPS = [[half * HALF + b for b in range(HALF)] for half in range(2)]


def dot(a, b, dims, precision=None):
    return lax.dot_general(
        a, b, (dims, ((), ())), precision=precision, preferred_element_type=F32
    )


def tile_of(row):
    return jnp.broadcast_to(row, (DH, DH)).T


class Tables:
    def __init__(self, decay_ref, doc_ref, start_ref):
        start = start_ref[0]
        rows = lax.broadcasted_iota(jnp.int32, (DH, DH), 0)
        cols = lax.broadcasted_iota(jnp.int32, (DH, DH), 1)
        self.causal = rows >= cols
        upto = self.causal.astype(F32)
        self.cum = dot(decay_ref[...], upto, ((1,), (1,)), HIGH)
        self.doc_row = doc_ref[...]
        self.doc = jnp.broadcast_to(self.doc_row, (DH, DH)).T
        self.doc_last = self.doc_row[:, DH - 1 : DH]
        self.start = start
        self.heads = self.cum.shape[0]

    def cum_row(self, h):
        return self.cum[h : h + 1, :]

    def last(self, h):
        return self.cum[h : h + 1, DH - 1 : DH]

    def decay(self, h):
        visible = (self.doc == self.doc_row) & self.causal
        spread = tile_of(self.cum_row(h)) - self.cum_row(h)
        return jnp.where(visible, jnp.exp(jnp.where(visible, spread, 0.0)), 0.0)

    def inward(self, h):
        return jnp.where(self.doc < self.start, jnp.exp(tile_of(self.cum_row(h))), 0.0)

    def outward(self, h):
        return jnp.where(
            self.doc == self.doc_last, jnp.exp(self.last(h) - tile_of(self.cum_row(h))), 0.0
        )

    def factor(self, h):
        gone = jnp.where(self.doc_last < self.start, jnp.exp(self.last(h)), 0.0)
        return jnp.broadcast_to(gone, (1, DH))


def split(x):
    high = x.astype(BF16)
    return high, (x - high.astype(F32)).astype(BF16)


def twice(x):
    return jnp.concatenate([x, x], axis=1)


def head(ref, h):
    return ref[:, h * DH : (h + 1) * DH]


def state(ref, h):
    return ref[h * DH : (h + 1) * DH, :]


def local_kernel(start_ref, key_ref, value_ref, decay_ref, doc_ref, local_ref, factor_ref):
    t = Tables(decay_ref, doc_ref, start_ref)
    for h in range(t.heads):
        weighted = (head(key_ref, h).astype(F32) * t.outward(h)).astype(BF16)
        local_ref[h * DH : (h + 1) * DH, :] = dot(weighted, head(value_ref, h), ((0,), (0,)))
        factor_ref[h : h + 1, :] = t.factor(h)


def inner_kernel(
    start_ref, query_ref, key_ref, value_ref, decay_ref, doc_ref, attend_ref, inner_ref
):
    t = Tables(decay_ref, doc_ref, start_ref)
    for h in range(t.heads):
        scores = dot(head(query_ref, h), head(key_ref, h), ((1,), (1,)))
        attend = (scores * t.decay(h)).astype(BF16)
        attend_ref[h * DH : (h + 1) * DH, :] = attend
        inner_ref[:, h * DH : (h + 1) * DH] = dot(attend, head(value_ref, h), ((1,), (0,)))


def pack_kernel(local_ref, factor_ref, edge_ref, packed_ref):
    for p in range(HALF):
        h = p * SUB // DH
        factor = factor_ref[h : h + 1, :]
        rows = pl.ds(p * SUB, SUB)
        at = p * (SUB + 1)
        packed_ref[at : at + SUB, :] = local_ref[rows, :] + factor * edge_ref[rows, :]
        packed_ref[at + SUB : at + SUB + 1, :] = factor


def forward_kernel(packed_ref, incoming_ref, factor_ref):
    carry = jnp.zeros((SUB, DH), F32)
    for b in range(HALF):
        at = b * (SUB + 1)
        rows = pl.ds(b * SUB, SUB)
        factor = jnp.broadcast_to(packed_ref[at + SUB : at + SUB + 1, :], (SUB, DH))
        incoming_ref[rows, :] = carry
        factor_ref[rows, :] = factor
        carry = factor * carry + packed_ref[at : at + SUB, :]


def backward_kernel(grad_ref, factor_ref, outgoing_ref):
    carry = jnp.zeros((SUB, DH), F32)
    for b in reversed(range(HALF)):
        rows = pl.ds(b * SUB, SUB)
        outgoing_ref[rows, :] = carry
        carry = factor_ref[rows, :] * carry + grad_ref[rows, :]


def output_kernel(
    start_ref,
    query_ref,
    grad_ref,
    gain_ref,
    decay_ref,
    doc_ref,
    inner_ref,
    incoming_ref,
    edge_ref,
    output_ref,
    state_ref,
    sums_ref,
):
    t = Tables(decay_ref, doc_ref, start_ref)
    square = jnp.zeros((DH, DH), F32)
    cross = jnp.zeros((DH, DH), F32)
    for h in range(t.heads):
        high, low = split(state(incoming_ref, h) + state(edge_ref, h))
        state_ref[h * DH : (h + 1) * DH, :] = jnp.concatenate([high, low], axis=1)
        stacked = jnp.concatenate([high, low], axis=0)
        carried = dot(twice(head(query_ref, h)), stacked, ((1,), (0,)))
        output = head(inner_ref, h) + t.inward(h) * carried
        output_ref[:, h * DH : (h + 1) * DH] = output
        scaled = head(grad_ref, h).astype(F32) * head(gain_ref, h)
        square = square + output * output
        cross = cross + scaled * output
    ones = jnp.ones((SUB, DH), F32)
    squares = dot(ones, square, ((1,), (1,)), HIGH)
    crosses = dot(ones, cross, ((1,), (1,)), HIGH)
    which = lax.broadcasted_iota(jnp.int32, (SUB, DH), 0)
    sums = jnp.where(which < SUB // 2, squares, crosses)
    for peer in range(sums_ref.shape[0] // SUB):
        sums_ref[peer * SUB : (peer + 1) * SUB, :] = sums


def grad_kernel(
    start_ref,
    query_ref,
    grad_ref,
    gain_ref,
    decay_ref,
    doc_ref,
    output_ref,
    sums_ref,
    normed_ref,
    grad_out_ref,
    grad_state_ref,
):
    t = Tables(decay_ref, doc_ref, start_ref)
    sums = sums_ref[0:SUB, :]
    for peer in range(1, sums_ref.shape[0] // SUB):
        sums = sums + sums_ref[peer * SUB : (peer + 1) * SUB, :]
    width = ATTN_GROUPS * DH
    inverse_row = lax.rsqrt(sums[0:1, :] / width + EPSILON)
    cross_row = sums[SUB // 2 : SUB // 2 + 1, :] / width
    inverse = tile_of(inverse_row)
    pull = tile_of(inverse_row * inverse_row * inverse_row * cross_row)
    for h in range(t.heads):
        gain = head(gain_ref, h)
        output = head(output_ref, h)
        scaled = head(grad_ref, h).astype(F32) * gain
        normed_ref[:, h * DH : (h + 1) * DH] = (output * inverse * gain).astype(BF16)
        grad_out = (inverse * scaled - output * pull).astype(BF16)
        grad_out_ref[:, h * DH : (h + 1) * DH] = grad_out
        gated = (head(query_ref, h).astype(F32) * t.inward(h)).astype(BF16)
        grad_state_ref[h * DH : (h + 1) * DH, :] = dot(gated, grad_out, ((0,), (0,)))


def edge_kernel(outgoing_ref, grad_state_ref, factor_ref, before_ref):
    for h in range(factor_ref.shape[0]):
        before_ref[h * DH : (h + 1) * DH, :] = (
            factor_ref[h : h + 1, :] * state(outgoing_ref, h) + state(grad_state_ref, h)
        )


def intra_kernel(
    start_ref,
    query_ref,
    key_ref,
    value_ref,
    decay_ref,
    doc_ref,
    grad_out_ref,
    attend_ref,
    state_ref,
    query_grad_ref,
    key_part_ref,
    value_part_ref,
):
    t = Tables(decay_ref, doc_ref, start_ref)
    for h in range(t.heads):
        grad_out = head(grad_out_ref, h)
        mixing = dot(grad_out, head(value_ref, h), ((1,), (1,))) * t.decay(h)
        mixing = mixing.astype(BF16)
        carried = dot(twice(grad_out), state(state_ref, h), ((1,), (1,)))
        query_grad = dot(mixing, head(key_ref, h), ((1,), (0,))) + t.inward(h) * carried
        query_grad_ref[:, h * DH : (h + 1) * DH] = query_grad.astype(BF16)
        key_part_ref[:, h * DH : (h + 1) * DH] = dot(mixing, head(query_ref, h), ((0,), (0,)))
        value_part_ref[:, h * DH : (h + 1) * DH] = dot(
            state(attend_ref, h), grad_out, ((0,), (0,))
        )


def final_kernel(
    start_ref,
    key_ref,
    value_ref,
    decay_ref,
    doc_ref,
    key_part_ref,
    value_part_ref,
    outgoing_ref,
    edge_ref,
    key_grad_ref,
    value_grad_ref,
):
    t = Tables(decay_ref, doc_ref, start_ref)
    for h in range(t.heads):
        high, low = split(state(outgoing_ref, h) + state(edge_ref, h))
        outward = t.outward(h)
        key_grad = head(key_part_ref, h) + outward * dot(
            twice(head(value_ref, h)), jnp.concatenate([high, low], axis=1), ((1,), (1,))
        )
        value_grad = head(value_part_ref, h) + outward * dot(
            twice(head(key_ref, h)), jnp.concatenate([high, low], axis=0), ((1,), (0,))
        )
        key_grad_ref[:, h * DH : (h + 1) * DH] = key_grad.astype(BF16)
        value_grad_ref[:, h * DH : (h + 1) * DH] = value_grad.astype(BF16)


def call(kernel, outs, *args, scalars=0):
    vmem = pl.BlockSpec(memory_space=pltpu.VMEM)
    smem = pl.BlockSpec(memory_space=pltpu.SMEM)
    return pl.pallas_call(
        kernel,
        out_shape=tuple(jax.ShapeDtypeStruct(shape, kind) for shape, kind in outs),
        in_specs=[smem] * scalars + [vmem] * (len(args) - scalars),
        out_specs=(vmem,) * len(outs),
        name=kernel.__name__,
    )(*args)


def exchange(rows, per_block):
    shape = (HALF, SUB, DH) if per_block == SUB else (HALF, per_block, 1, DH)
    moved = lax.all_to_all(
        rows.reshape(shape), "ctx", 0, 0, axis_index_groups=GROUPS, tiled=True
    )
    return moved.reshape(rows.shape)


def on_device(queries, key_rows, value_rows, out_grad, log_decay, doc_start, norm_gain):
    tokens, width = queries.shape
    heads = width // DH
    start = (lax.axis_index("ctx") * tokens).astype(jnp.int32).reshape(1)
    docs = doc_start.reshape(1, tokens)
    gains = norm_gain.reshape(1, width)
    states = ((heads * DH, DH), F32)
    wide = ((tokens, width), F32)
    narrow = ((tokens, width), BF16)
    decays = (log_decay, docs)

    local, factor = call(
        local_kernel, (states, ((heads, DH), F32)), start, key_rows, value_rows, *decays, scalars=1
    )
    edge = lax.ppermute(local, "ctx", [(HALF - 1, HALF)])
    attend, inner = call(
        inner_kernel,
        (((heads * DH, DH), BF16), wide),
        start,
        queries,
        key_rows,
        value_rows,
        *decays,
        scalars=1,
    )
    (packed,) = call(pack_kernel, (((HALF * (SUB + 1), DH), F32),), local, factor, edge)
    packed = exchange(packed, SUB + 1)
    incoming, factors = call(
        forward_kernel, (((HALF * SUB, DH), F32), ((HALF * SUB, DH), F32)), packed
    )
    incoming = exchange(incoming, SUB)

    peers = lax.axis_size("head")
    output, inbound, sums = call(
        output_kernel,
        (wide, ((heads * DH, 2 * DH), BF16), ((peers * SUB, DH), F32)),
        start,
        queries,
        out_grad,
        gains,
        *decays,
        inner,
        incoming,
        edge,
        scalars=1,
    )
    sums = lax.all_to_all(sums.reshape(peers, SUB, DH), "head", 0, 0, tiled=True)
    normed, grad_out, grad_state = call(
        grad_kernel,
        (narrow, narrow, states),
        start,
        queries,
        out_grad,
        gains,
        *decays,
        output,
        sums.reshape(peers * SUB, DH),
        scalars=1,
    )

    arrived = exchange(grad_state, SUB)
    (outgoing,) = call(backward_kernel, (((HALF * SUB, DH), F32),), arrived, factors)
    outgoing = exchange(outgoing, SUB)
    (before,) = call(edge_kernel, (states,), outgoing, grad_state, factor)
    after = lax.ppermute(before, "ctx", [(HALF, HALF - 1)])
    query_grad, key_part, value_part = call(
        intra_kernel,
        (narrow, wide, wide),
        start,
        queries,
        key_rows,
        value_rows,
        *decays,
        grad_out,
        attend,
        inbound,
        scalars=1,
    )
    key_grad, value_grad = call(
        final_kernel,
        (narrow, narrow),
        start,
        key_rows,
        value_rows,
        *decays,
        key_part,
        value_part,
        outgoing,
        after,
        scalars=1,
    )
    return normed, query_grad, key_grad, value_grad


def solution(mesh):
    rows = P("ctx", "head")
    return jax.shard_map(
        on_device,
        mesh=mesh,
        in_specs=(rows, rows, rows, rows, P("head", "ctx"), P("ctx"), P("head")),
        out_specs=(rows, rows, rows, rows),
        check_vma=False,
    )
```

time: 747 us -> 130 us (0.17); the launches traced: 739 us -> 129 us
  other arithmetic: 276 us -> 0 us
  blocking collectives: 279 us -> 86.9 us
  waiting for transfers between devices: 144 us -> 9.48 us
  Pallas kernels: 0 us -> 23.4 us
  between operations: 15.5 us -> 0.69 us
  loops' own time: 9.66 us -> 0 us
  local copies, waits for them, and re-layouts: 9.97 us -> 2.12 us
    select_n x256 -> x0, other arithmetic: 270 us -> none  [turn(): return jax.tree.map(lambda a, b: jnp.where(reached, a, b), new, before)]
    unnamed x1 -> x0, blocking collectives: 266 us -> none
    all_gather x2 -> x0, waiting for transfers between devices: 144 us -> none  [prefix(): everything = jax.tree.map(lambda part: lax.all_gather(part, axis), array)]
    all_to_all x0 -> x4, blocking collectives: none -> 86.9 us  [the longest x3 73.4 us: exchange(): lax.all_to_all(rows.reshape(shape), 'ctx', 0, 0, axis_index_groups=GROUPS...]
    pallas_call x0 -> x10, Pallas kernels: none -> 23.4 us  [call(): pl.pallas_call(kernel, out_shape=tuple((jax.ShapeDtypeStruct(shape, kind)...]
    psum x1 -> x0, blocking collectives: 13.5 us -> none  [on_device(): lax.psum((jnp.sum(output * output, axis=1), jnp.sum(scaled_grad * output,...]
    another operation x2 -> x0, loops' own time: 9.66 us -> none  [prefix(): return lax.fori_loop(0, peers, turn, start)]
    all_to_all x0 -> x1, waiting for transfers between devices: none -> 9.47 us  [exchange(): lax.all_to_all(rows.reshape(shape), 'ctx', 0, 0, axis_index_groups=GROUPS...]
  transfers between devices with their start and end apart: 2 -> 3, of which waited for: 1 -> 1; matrix products, arithmetic and copies ran while one was open for 1% -> 0% of each run, Pallas kernels for 0% -> 5%
where the time goes in v1:
time: 130 us; the launch traced here: 129 us
  blocking collectives  86.9 us (67%)
  Pallas kernels  23.4 us (18%)
  waiting for transfers between devices  9.48 us (7%)
  starting transfers between devices  6.84 us (5%)
  local copies, waits for them, and re-layouts  2.12 us (2%)
    all_to_all x3, blocking collectives, exchange(): lax.all_to_all(rows.reshape(shape), 'ctx', 0, 0, axis_index_groups=GROUPS...  73.4 us
    pallas_call x10, Pallas kernels, call(): pl.pallas_call(kernel, out_shape=tuple((jax.ShapeDtypeStruct(shape, kind)...  23.4 us
    all_to_all x1, blocking collectives, on_device(): lax.all_to_all(sums.reshape(peers, SUB, DH), 'head', 0, 0, tiled=True)  13.5 us
    all_to_all x1, waiting for transfers between devices, exchange(): lax.all_to_all(rows.reshape(shape), 'ctx', 0, 0, axis_index_groups=GROUPS...  9.47 us
    all_to_all x1, starting transfers between devices, exchange(): lax.all_to_all(rows.reshape(shape), 'ctx', 0, 0, axis_index_groups=GROUPS...  5.51 us
  transfers between devices with their start and end apart: 3, of which 1 were waited for; matrix products, arithmetic and copies ran while one was open for 0% of the time, Pallas kernels for 5%

profile of v1, /device:TPU:1, one launch (start us, length us, event | category | flops | bytes accessed | tf_op | source)
XLA Modules:
  0.0 129.4 jit_solution(12336274079872006667)
XLA Ops:
  0.6 2.3 %local_kernel.1 = (f32[512,128]{1,0:T(8,128)}, f32[4,128]{1,0:T(4,128)}) custom-call(s32[1]{0:T(128)} %bitcast.start_ref, bf16[128,512]{1,0:T(8,128)(2,1)} %key_ref.7, bf16[128,512]{1,0:T(8,128)(2,1)} %value_ref.7, f32[4,128]{1,0:T(4,128)} %decay_ref.11, s32[1,128]{1,0:T(1,128)} %bitcast.24), custom_call_target="tpu_custom_call" | custom-call | tf_op jit(solution)/shard_map/local_kernel/pallas_call | solution.py:267
  3.0 0.7 collective-permute-start
  3.6 0.0 collective-permute-done.edge_ref
  3.6 0.0 copy-start
  3.7 0.7 copy-done
  4.4 1.8 %pack_kernel.1 = f32[576,128]{1,0:T(8,128)} custom-call(f32[512,128]{1,0:T(8,128)} %get-tuple-element.22.local_ref, f32[4,128]{1,0:T(4,128)} %get-tuple-element.23.factor_ref, f32[512,128]{1,0:T(8,128)} %copy-done), custom_call_target="tpu_custom_call" | custom-call | tf_op jit(solution)/shard_map/pack_kernel/pallas_call | solution.py:267
  6.2 36.2 %all_to_all.25 = f32[64,9,1,128]{3,2,1,0:T(1,128)} all-to-all(f32[64,9,1,128]{3,2,1,0:T(1,128)} %bitcast.15), channel_id=1, replica_groups={{0,8,16,24,32,40,48,56,64,72,80,88,96,104,112,120,128,136,144,152,160,1..., dimensions={0} | all-to-all | bytes 589824 | tf_op jit(solution)/shard_map/all_to_all | solution.py:278
  42.3 1.8 %forward_kernel.1 = (f32[512,128]{1,0:T(8,128)}, f32[512,128]{1,0:T(8,128)}) custom-call(f32[576,128]{1,0:T(8,128)} %bitcast.16), custom_call_target="tpu_custom_call" | custom-call | tf_op jit(solution)/shard_map/forward_kernel/pallas_call | solution.py:267
  44.1 5.5 %all-to-all-start.1 = ((f32[64,8,128]{2,1,0:T(8,128)}), f32[64,8,128]{2,1,0:T(8,128)S(1)}, u32[]{:S(2)}, u32[]{:S(2)}) async-start(f32[64,8,128]{2,1,0:T(8,128)} %bitcast.21), calls=%async_computation.1 | async-start | bytes 524288 | tf_op jit(solution)/shard_map/all_to_all | solution.py:278
  49.6 2.8 %inner_kernel.1 = (bf16[512,128]{1,0:T(8,128)(2,1)}, f32[128,512]{1,0:T(8,128)}) custom-call(s32[1]{0:T(128)} %bitcast.start_ref, bf16[128,512]{1,0:T(8,128)(2,1)} %query_ref.7, bf16[128,512]{1,0:T(8,128)(2,1)} %key_ref.7, bf16[128,512]{1,0:T(8,128)(2,1)} %value_ref.7, f32[4,128]{1,0:T(4,128)} %decay_ref.11, s32[1,128]{1,0:T(1,128)} %bitcast.25), custom_call_target="tpu_custom_call" | custom-call | tf_op jit(solution)/shard_map/inner_kernel/pallas_call | solution.py:267
  52.4 9.5 %all-to-all-done.1 = f32[64,8,128]{2,1,0:T(8,128)S(1)} async-done(((f32[64,8,128]{2,1,0:T(8,128)}), f32[64,8,128]{2,1,0:T(8,128)S(1)}, u32[]{:S(2)}, u32[]{:S(2)}) %all-to-all-start.1) | async-done | bytes 262176 | tf_op jit(solution)/shard_map/all_to_all | solution.py:278
  61.9 0.0 copy-start.1
  61.9 0.7 copy-done.1
  62.6 2.7 %output_kernel.1 = (f32[128,512]{1,0:T(8,128)}, bf16[512,256]{1,0:T(8,128)(2,1)}, f32[64,128]{1,0:T(8,128)}) custom-call(s32[1]{0:T(128)} %bitcast.start_ref, bf16[128,512]{1,0:T(8,128)(2,1)} %query_ref.7, bf16[128,512]{1,0:T(8,128)(2,1)} %grad_ref.3, f32[1,512]{1,0:T(1,128)} %bitcast.30, f32[4,128]{1,0:T(4,128)} %decay_ref.11, s32[1,128]{1,0:T(1,128)} %bitcast.26, ...), custom_call_target="tpu_custom_call" | custom-call | tf_op jit(solution)/shard_map/output_kernel/pallas_call | solution.py:267
  65.3 13.5 %all_to_all.26 = f32[8,8,128]{2,1,0:T(8,128)} all-to-all(f32[8,8,128]{2,1,0:T(8,128)} %bitcast.23), channel_id=1, replica_groups=mesh['ctx'=128,'head'=8] {'head'}, dimensions={0} | all-to-all | bytes 65536 | tf_op jit(solution)/shard_map/all_to_all | solution.py:330
  78.8 2.4 %grad_kernel.1 = (bf16[128,512]{1,0:T(8,128)(2,1)}, bf16[128,512]{1,0:T(8,128)(2,1)}, f32[512,128]{1,0:T(8,128)}) custom-call(s32[1]{0:T(128)} %bitcast.start_ref, bf16[128,512]{1,0:T(8,128)(2,1)} %query_ref.7, bf16[128,512]{1,0:T(8,128)(2,1)} %grad_ref.3, f32[1,512]{1,0:T(1,128)} %bitcast.31, f32[4,128]{1,0:T(4,128)} %decay_ref.11, s32[1,128]{1,0:T(1,128)} %bitcast.27, ...), custom_call_target="tpu_custom_call" | custom-call | tf_op jit(solution)/shard_map/grad_kernel/pallas_call | solution.py:267
  81.1 19.4 %all_to_all.27 = f32[64,8,128]{2,1,0:T(8,128)} all-to-all(f32[64,8,128]{2,1,0:T(8,128)} %bitcast.18), channel_id=1, replica_groups={{0,8,16,24,32,40,48,56,64,72,80,88,96,104,112,120,128,136,144,152,160,1..., dimensions={0} | all-to-all | bytes 524288 | tf_op jit(solution)/shard_map/all_to_all | solution.py:278
  100.5 1.9 %backward_kernel.1 = f32[512,128]{1,0:T(8,128)} custom-call(f32[512,128]{1,0:T(8,128)} %bitcast.19, f32[512,128]{1,0:T(8,128)} %get-tuple-element.35.factor_ref), custom_call_target="tpu_custom_call" | custom-call | tf_op jit(solution)/shard_map/backward_kernel/pallas_call | solution.py:267
  102.4 17.9 %all_to_all.28 = f32[64,8,128]{2,1,0:T(8,128)} all-to-all(f32[64,8,128]{2,1,0:T(8,128)} %bitcast.20), channel_id=1, replica_groups={{0,8,16,24,32,40,48,56,64,72,80,88,96,104,112,120,128,136,144,152,160,1..., dimensions={0} | all-to-all | bytes 524288 | tf_op jit(solution)/shard_map/all_to_all | solution.py:278
  120.3 1.8 %edge_kernel.1 = f32[512,128]{1,0:T(8,128)} custom-call(f32[512,128]{1,0:T(8,128)} %bitcast.13, f32[512,128]{1,0:T(8,128)} %get-tuple-element.34.grad_state_ref, f32[4,128]{1,0:T(4,128)} %get-tuple-element.23.factor_ref), custom_call_target="tpu_custom_call" | custom-call | tf_op jit(solution)/shard_map/edge_kernel/pallas_call | solution.py:267
  122.1 0.7 collective-permute-start.1
  122.7 3.4 %intra_kernel.1 = (bf16[128,512]{1,0:T(8,128)(2,1)}, f32[128,512]{1,0:T(8,128)}, f32[128,512]{1,0:T(8,128)}) custom-call(s32[1]{0:T(128)} %bitcast.start_ref, bf16[128,512]{1,0:T(8,128)(2,1)} %query_ref.7, bf16[128,512]{1,0:T(8,128)(2,1)} %key_ref.7, bf16[128,512]{1,0:T(8,128)(2,1)} %value_ref.7, f32[4,128]{1,0:T(4,128)} %decay_ref.11, s32[1,128]{1,0:T(1,128)} %bitcast.28, ...), custom_call_target="tpu_custom_call" | custom-call | tf_op jit(solution)/shard_map/intra_kernel/pallas_call | solution.py:267
  126.1 0.0 collective-permute-done.1.edge_ref
  126.1 0.0 copy-start.2
  126.1 0.7 copy-done.2
  126.8 2.6 %final_kernel.1 = (bf16[128,512]{1,0:T(8,128)(2,1)}, bf16[128,512]{1,0:T(8,128)(2,1)}) custom-call(s32[1]{0:T(128)} %bitcast.start_ref, bf16[128,512]{1,0:T(8,128)(2,1)} %key_ref.7, bf16[128,512]{1,0:T(8,128)(2,1)} %value_ref.7, f32[4,128]{1,0:T(4,128)} %decay_ref.11, s32[1,128]{1,0:T(1,128)} %bitcast.29, f32[128,512]{1,0:T(8,128)} %get-tuple-element.32.key_part_ref, ...), custom_call_target="tpu_custom_call" | custom-call | tf_op jit(solution)/shard_map/final_kernel/pallas_call | solution.py:267
Async XLA Ops:
  3.0 0.7 collective-permute-start
  3.6 0.7 copy-start
  44.1 17.8 %all-to-all-start.1 = ((f32[64,8,128]{2,1,0:T(8,128)}), f32[64,8,128]{2,1,0:T(8,128)S(1)}, u32[]{:S(2)}, u32[]{:S(2)}) async-start(f32[64,8,128]{2,1,0:T(8,128)} %bitcast.21), calls=%async_computation.1 | async-start | bytes 524288 | tf_op jit(solution)/shard_map/all_to_all | solution.py:278
  61.9 0.7 copy-start.1
  122.1 4.0 %collective-permute-start.1 = (f32[512,128]{1,0:T(8,128)}, f32[512,128]{1,0:T(8,128)S(1)}, u32[]{:S(2)}, u32[]{:S(2)}) collective-permute-start(f32[512,128]{1,0:T(8,128)} %edge_kernel.1), channel_id=1, source_target_pairs={{512,504},{513,505},{514,506},{515,507},{516,508},{517,509},{518,5... | collective-permute-start | bytes 786440 | tf_op jit(solution)/shard_map/ppermute | solution.py:348
  126.1 0.7 copy-start.2

commit v2 on v1

--- a/solution.py
+++ b/solution.py
@@ -266,11 +266,14 @@
     smem = pl.BlockSpec(memory_space=pltpu.SMEM)
     return pl.pallas_call(
         kernel,
-        out_shape=tuple(jax.ShapeDtypeStruct(shape, kind) for shape, kind in outs),
+        out_shape=tuple(
+            pltpu.VMEM(shape, kind) if keep else jax.ShapeDtypeStruct(shape, kind)
+            for shape, kind, *keep in outs
+        ),
         in_specs=[smem] * scalars + [vmem] * (len(args) - scalars),
         out_specs=(vmem,) * len(outs),
         name=kernel.__name__,
-    )(*args)
+    )(*args[:scalars], *(pltpu.with_memory_space_constraint(x, pltpu.VMEM) for x in args[scalars:]))
 
 
 def exchange(rows, per_block):
@@ -287,18 +290,18 @@
     start = (lax.axis_index("ctx") * tokens).astype(jnp.int32).reshape(1)
     docs = doc_start.reshape(1, tokens)
     gains = norm_gain.reshape(1, width)
-    states = ((heads * DH, DH), F32)
-    wide = ((tokens, width), F32)
+    states = ((heads * DH, DH), F32, True)
+    wide = ((tokens, width), F32, True)
     narrow = ((tokens, width), BF16)
     decays = (log_decay, docs)
 
     local, factor = call(
-        local_kernel, (states, ((heads, DH), F32)), start, key_rows, value_rows, *decays, scalars=1
+        local_kernel, (states, ((heads, DH), F32, True)), start, key_rows, value_rows, *decays, scalars=1
     )
     edge = lax.ppermute(local, "ctx", [(HALF - 1, HALF)])
     attend, inner = call(
         inner_kernel,
-        (((heads * DH, DH), BF16), wide),
+        (((heads * DH, DH), BF16, True), wide),
         start,
         queries,
         key_rows,
@@ -306,17 +309,17 @@
         *decays,
         scalars=1,
     )
-    (packed,) = call(pack_kernel, (((HALF * (SUB + 1), DH), F32),), local, factor, edge)
+    (packed,) = call(pack_kernel, (((HALF * (SUB + 1), DH), F32, True),), local, factor, edge)
     packed = exchange(packed, SUB + 1)
     incoming, factors = call(
-        forward_kernel, (((HALF * SUB, DH), F32), ((HALF * SUB, DH), F32)), packed
+        forward_kernel, (((HALF * SUB, DH), F32, True), ((HALF * SUB, DH), F32, True)), packed
     )
     incoming = exchange(incoming, SUB)
 
     peers = lax.axis_size("head")
     output, inbound, sums = call(
         output_kernel,
-        (wide, ((heads * DH, 2 * DH), BF16), ((peers * SUB, DH), F32)),
+        (wide, ((heads * DH, 2 * DH), BF16, True), ((peers * SUB, DH), F32, True)),
         start,
         queries,
         out_grad,
@@ -330,7 +333,7 @@
     sums = lax.all_to_all(sums.reshape(peers, SUB, DH), "head", 0, 0, tiled=True)
     normed, grad_out, grad_state = call(
         grad_kernel,
-        (narrow, narrow, states),
+        (narrow, (*narrow, True), states),
         start,
         queries,
         out_grad,
@@ -342,7 +345,7 @@
     )
 
     arrived = exchange(grad_state, SUB)
-    (outgoing,) = call(backward_kernel, (((HALF * SUB, DH), F32),), arrived, factors)
+    (outgoing,) = call(backward_kernel, (((HALF * SUB, DH), F32, True),), arrived, factors)
     outgoing = exchange(outgoing, SUB)
     (before,) = call(edge_kernel, (states,), outgoing, grad_state, factor)
     after = lax.ppermute(before, "ctx", [(HALF, HALF - 1)])

time: 130 us -> 115 us (0.88)
  Pallas kernels: 23.4 us -> 7.48 us
  blocking collectives: 86.9 us -> 85.1 us
  waiting for transfers between devices: 9.48 us -> 11.2 us
    pallas_call x10, Pallas kernels: 23.4 us -> 7.48 us  [call(): pl.pallas_call(kernel, out_shape=tuple((pltpu.VMEM(shape, kind) if keep e...]
    all_to_all x1, waiting for transfers between devices: 9.47 us -> 11.2 us  [exchange(): lax.all_to_all(rows.reshape(shape), 'ctx', 0, 0, axis_index_groups=GROUPS...]
    all_to_all x3, blocking collectives: 73.4 us -> 71.9 us  [exchange(): lax.all_to_all(rows.reshape(shape), 'ctx', 0, 0, axis_index_groups=GROUPS...]
    unnamed x6 -> x18, local copies, waits for them, and re-layouts: 2.12 us -> 3.17 us
  transfers between devices with their start and end apart: 3 -> 3, of which waited for: 1 -> 1; matrix products, arithmetic and copies ran while one was open for 0% -> 0% of each run, Pallas kernels for 5% -> 2%
where the time goes in v2:
time: 115 us
  blocking collectives  85.1 us (74%)
  waiting for transfers between devices  11.2 us (10%)
  Pallas kernels  7.48 us (7%)
  starting transfers between devices  7 us (6%)
  local copies, waits for them, and re-layouts  3.17 us (3%)
    all_to_all x3, blocking collectives, exchange(): lax.all_to_all(rows.reshape(shape), 'ctx', 0, 0, axis_index_groups=GROUPS...  71.9 us
    all_to_all x1, blocking collectives, on_device(): lax.all_to_all(sums.reshape(peers, SUB, DH), 'head', 0, 0, tiled=True)  13.2 us
    all_to_all x1, waiting for transfers between devices, exchange(): lax.all_to_all(rows.reshape(shape), 'ctx', 0, 0, axis_index_groups=GROUPS...  11.2 us
    pallas_call x10, Pallas kernels, call(): pl.pallas_call(kernel, out_shape=tuple((pltpu.VMEM(shape, kind) if keep e...  7.48 us
    all_to_all x1, starting transfers between devices, exchange(): lax.all_to_all(rows.reshape(shape), 'ctx', 0, 0, axis_index_groups=GROUPS...  5.64 us
    unnamed x18, local copies, waits for them, and re-layouts  3.17 us
  transfers between devices with their start and end apart: 3, of which 1 were waited for; matrix products, arithmetic and copies ran while one was open for 0% of the time, Pallas kernels for 2%

profile of v2, /device:TPU:1, one launch (start us, length us, event | category | flops | bytes accessed | tf_op | source)
XLA Modules:
  0.0 114.7 jit_solution(11979364675668826368)
XLA Ops:
  0.6 0.0 copy-start.6
  0.6 0.0 copy-start.7
  0.7 0.7 copy-done.6
  1.3 0.0 copy-done.7
  1.3 0.0 copy-start.1
  1.3 0.9 copy-done.1
  2.2 0.0 copy-start.3
  2.2 0.9 copy-done.3
  3.1 0.6 local_kernel.1
  3.8 0.7 collective-permute-start
  4.4 0.0 collective-permute-done.edge_ref
  4.5 0.1 pack_kernel.1
  4.5 35.6 %all_to_all.25 = f32[64,9,1,128]{3,2,1,0:T(1,128)S(1)} all-to-all(f32[64,9,1,128]{3,2,1,0:T(1,128)S(1)} %bitcast.15), channel_id=1, replica_groups={{0,8,16,24,32,40,48,56,64,72,80,88,96,104,112,120,128,136,144,152,160,1..., dimensions={0} | all-to-all | bytes 589824 | tf_op jit(solution)/shard_map/all_to_all | solution.py:281
  40.1 0.8 forward_kernel.1
  40.9 0.0 copy-start
  40.9 0.0 copy-start.2
  40.9 0.0 copy-start.4
  40.9 5.6 %all-to-all-start.1 = ((f32[64,8,128]{2,1,0:T(8,128)}), f32[64,8,128]{2,1,0:T(8,128)S(1)}, u32[]{:S(2)}, u32[]{:S(2)}) async-start(f32[64,8,128]{2,1,0:T(8,128)} %bitcast.5), calls=%async_computation.1 | async-start | bytes 524288 | tf_op jit(solution)/shard_map/all_to_all | solution.py:281
  46.6 0.0 copy-done
  46.6 0.0 copy-done.2
  46.6 0.0 copy-done.4
  46.6 0.0 copy-start.5
  46.6 1.0 inner_kernel.1
  47.6 11.2 %all-to-all-done.1 = f32[64,8,128]{2,1,0:T(8,128)S(1)} async-done(((f32[64,8,128]{2,1,0:T(8,128)}), f32[64,8,128]{2,1,0:T(8,128)S(1)}, u32[]{:S(2)}, u32[]{:S(2)}) %all-to-all-start.1) | async-done | bytes 262176 | tf_op jit(solution)/shard_map/all_to_all | solution.py:281
  58.8 0.0 copy-start.8
  58.8 0.0 copy-done.5
  58.8 0.7 copy-done.8
  59.5 0.8 output_kernel.1
  60.3 13.2 %all_to_all.26 = f32[8,8,128]{2,1,0:T(8,128)S(1)} all-to-all(f32[8,8,128]{2,1,0:T(8,128)S(1)} %bitcast.22), channel_id=1, replica_groups=mesh['ctx'=128,'head'=8] {'head'}, dimensions={0} | all-to-all | bytes 65536 | tf_op jit(solution)/shard_map/all_to_all | solution.py:333
  73.4 0.9 grad_kernel.1
  74.4 18.9 %all_to_all.27 = f32[64,8,128]{2,1,0:T(8,128)S(1)} all-to-all(f32[64,8,128]{2,1,0:T(8,128)S(1)} %bitcast.18), channel_id=1, replica_groups={{0,8,16,24,32,40,48,56,64,72,80,88,96,104,112,120,128,136,144,152,160,1..., dimensions={0} | all-to-all | bytes 524288 | tf_op jit(solution)/shard_map/all_to_all | solution.py:281
  93.3 0.1 backward_kernel.1
  93.4 17.5 %all_to_all.28 = f32[64,8,128]{2,1,0:T(8,128)S(1)} all-to-all(f32[64,8,128]{2,1,0:T(8,128)S(1)} %bitcast.20), channel_id=1, replica_groups={{0,8,16,24,32,40,48,56,64,72,80,88,96,104,112,120,128,136,144,152,160,1..., dimensions={0} | all-to-all | bytes 524288 | tf_op jit(solution)/shard_map/all_to_all | solution.py:281
  110.9 0.7 collective-permute-start.1
  111.6 1.9 %intra_kernel.1 = (bf16[128,512]{1,0:T(8,128)(2,1)}, f32[128,512]{1,0:T(8,128)S(1)}, f32[128,512]{1,0:T(8,128)S(1)}) custom-call(s32[1]{0:T(128)} %bitcast.start_ref, bf16[128,512]{1,0:T(8,128)(2,1)S(1)} %copy-done, bf16[128,512]{1,0:T(8,128)(2,1)S(1)} %copy-done.2, bf16[128,512]{1,0:T(8,128)(2,1)S(1)} %copy-done.4, f32[4,128]{1,0:T(4,128)S(1)} %copy-done.6, ...), custom_call_target="tpu_custom_call" | custom-call | tf_op jit(solution)/shard_map/intra_kernel/pallas_call | solution.py:267
  113.5 0.0 collective-permute-done.1.edge_ref
  113.5 1.2 %final_kernel.1 = (bf16[128,512]{1,0:T(8,128)(2,1)}, bf16[128,512]{1,0:T(8,128)(2,1)}) custom-call(s32[1]{0:T(128)} %bitcast.start_ref, bf16[128,512]{1,0:T(8,128)(2,1)S(1)} %copy-done.2, bf16[128,512]{1,0:T(8,128)(2,1)S(1)} %copy-done.4, f32[4,128]{1,0:T(4,128)S(1)} %copy-done.6, s32[1,128]{1,0:T(1,128)S(1)} %bitcast.28, ...), custom_call_target="tpu_custom_call" | custom-call | tf_op jit(solution)/shard_map/final_kernel/pallas_call | solution.py:267
  (1 shorter events, 0.0 us)
Async XLA Ops:
  0.6 0.7 copy-start.6
  0.6 0.7 copy-start.7
  1.3 0.9 copy-start.1
  2.2 0.9 copy-start.3
  3.8 0.7 collective-permute-start
  40.9 5.7 %copy-start = (bf16[128,512]{1,0:T(8,128)(2,1)S(1)}, bf16[128,512]{1,0:T(8,128)(2,1)}, u32[]{:S(2)}) copy-start(bf16[128,512]{1,0:T(8,128)(2,1)} %query_ref.7) | copy-start | bytes 393220
  40.9 5.7 %copy-start.2 = (bf16[128,512]{1,0:T(8,128)(2,1)S(1)}, bf16[128,512]{1,0:T(8,128)(2,1)}, u32[]{:S(2)}) copy-start(bf16[128,512]{1,0:T(8,128)(2,1)} %key_ref.7) | copy-start | bytes 393220
  40.9 5.7 %copy-start.4 = (bf16[128,512]{1,0:T(8,128)(2,1)S(1)}, bf16[128,512]{1,0:T(8,128)(2,1)}, u32[]{:S(2)}) copy-start(bf16[128,512]{1,0:T(8,128)(2,1)} %value_ref.7) | copy-start | bytes 393220
  40.9 17.9 %all-to-all-start.1 = ((f32[64,8,128]{2,1,0:T(8,128)}), f32[64,8,128]{2,1,0:T(8,128)S(1)}, u32[]{:S(2)}, u32[]{:S(2)}) async-start(f32[64,8,128]{2,1,0:T(8,128)} %bitcast.5), calls=%async_computation.1 | async-start | bytes 524288 | tf_op jit(solution)/shard_map/all_to_all | solution.py:281
  46.6 12.2 %copy-start.5 = (bf16[128,512]{1,0:T(8,128)(2,1)S(1)}, bf16[128,512]{1,0:T(8,128)(2,1)}, u32[]{:S(2)}) copy-start(bf16[128,512]{1,0:T(8,128)(2,1)} %grad_ref.3) | copy-start | bytes 393220
  58.8 0.7 copy-start.8
  110.9 2.6 %collective-permute-start.1 = (f32[512,128]{1,0:T(8,128)S(1)}, f32[512,128]{1,0:T(8,128)S(1)}, u32[]{:S(2)}, u32[]{:S(2)}) collective-permute-start(f32[512,128]{1,0:T(8,128)S(1)} %edge_kernel.1), channel_id=1, source_target_pairs={{512,504},{513,505},{514,506},{515,507},{516,508},{517,509},{518,5... | collective-permute-start | bytes 786440 | tf_op jit(solution)/shard_map/ppermute | solution.py:351

commit v3 on v2

--- a/solution.py
+++ b/solution.py
@@ -91,12 +91,29 @@
 
 
 def inner_kernel(
-    start_ref, query_ref, key_ref, value_ref, decay_ref, doc_ref, attend_ref, inner_ref
+    start_ref,
+    query_ref,
+    key_ref,
+    value_ref,
+    grad_ref,
+    gain_ref,
+    decay_ref,
+    doc_ref,
+    attend_ref,
+    inner_ref,
+    inward_ref,
+    gated_ref,
+    scaled_ref,
 ):
     t = Tables(decay_ref, doc_ref, start_ref)
     for h in range(t.heads):
+        decay = t.decay(h)
+        inward = t.inward(h)
+        inward_ref[h * DH : (h + 1) * DH, :] = inward
+        gated_ref[:, h * DH : (h + 1) * DH] = (head(query_ref, h).astype(F32) * inward).astype(BF16)
+        scaled_ref[:, h * DH : (h + 1) * DH] = head(grad_ref, h).astype(F32) * head(gain_ref, h)
         scores = dot(head(query_ref, h), head(key_ref, h), ((1,), (1,)))
-        attend = (scores * t.decay(h)).astype(BF16)
+        attend = (scores * decay).astype(BF16)
         attend_ref[h * DH : (h + 1) * DH, :] = attend
         inner_ref[:, h * DH : (h + 1) * DH] = dot(attend, head(value_ref, h), ((1,), (0,)))
 
@@ -131,12 +148,9 @@
 
 
 def output_kernel(
-    start_ref,
     query_ref,
-    grad_ref,
-    gain_ref,
-    decay_ref,
-    doc_ref,
+    scaled_ref,
+    inward_ref,
     inner_ref,
     incoming_ref,
     edge_ref,
@@ -144,19 +158,17 @@
     state_ref,
     sums_ref,
 ):
-    t = Tables(decay_ref, doc_ref, start_ref)
     square = jnp.zeros((DH, DH), F32)
     cross = jnp.zeros((DH, DH), F32)
-    for h in range(t.heads):
+    for h in range(query_ref.shape[1] // DH):
         high, low = split(state(incoming_ref, h) + state(edge_ref, h))
         state_ref[h * DH : (h + 1) * DH, :] = jnp.concatenate([high, low], axis=1)
         stacked = jnp.concatenate([high, low], axis=0)
         carried = dot(twice(head(query_ref, h)), stacked, ((1,), (0,)))
-        output = head(inner_ref, h) + t.inward(h) * carried
+        output = head(inner_ref, h) + state(inward_ref, h) * carried
         output_ref[:, h * DH : (h + 1) * DH] = output
-        scaled = head(grad_ref, h).astype(F32) * head(gain_ref, h)
         square = square + output * output
-        cross = cross + scaled * output
+        cross = cross + head(scaled_ref, h) * output
     ones = jnp.ones((SUB, DH), F32)
     squares = dot(ones, square, ((1,), (1,)), HIGH)
     crosses = dot(ones, cross, ((1,), (1,)), HIGH)
@@ -166,37 +178,31 @@
         sums_ref[peer * SUB : (peer + 1) * SUB, :] = sums
 
 
-def grad_kernel(
-    start_ref,
-    query_ref,
-    grad_ref,
-    gain_ref,
-    decay_ref,
-    doc_ref,
-    output_ref,
-    sums_ref,
-    normed_ref,
-    grad_out_ref,
-    grad_state_ref,
-):
-    t = Tables(decay_ref, doc_ref, start_ref)
+def scales(sums_ref):
     sums = sums_ref[0:SUB, :]
     for peer in range(1, sums_ref.shape[0] // SUB):
         sums = sums + sums_ref[peer * SUB : (peer + 1) * SUB, :]
     width = ATTN_GROUPS * DH
-    inverse_row = lax.rsqrt(sums[0:1, :] / width + EPSILON)
-    cross_row = sums[SUB // 2 : SUB // 2 + 1, :] / width
-    inverse = tile_of(inverse_row)
-    pull = tile_of(inverse_row * inverse_row * inverse_row * cross_row)
-    for h in range(t.heads):
-        gain = head(gain_ref, h)
-        output = head(output_ref, h)
-        scaled = head(grad_ref, h).astype(F32) * gain
-        normed_ref[:, h * DH : (h + 1) * DH] = (output * inverse * gain).astype(BF16)
-        grad_out = (inverse * scaled - output * pull).astype(BF16)
+    inverse = lax.rsqrt(sums[0:1, :] / width + EPSILON)
+    cross = sums[SUB // 2 : SUB // 2 + 1, :] / width
+    return tile_of(inverse), tile_of(inverse * inverse * inverse * cross)
+
+
+def grad_kernel(
+    scaled_ref,
+    gated_ref,
+    output_ref,
+    sums_ref,
+    grad_out_ref,
+    grad_state_ref,
+):
+    inverse, pull = scales(sums_ref)
+    for h in range(scaled_ref.shape[1] // DH):
+        grad_out = (inverse * head(scaled_ref, h) - head(output_ref, h) * pull).astype(BF16)
         grad_out_ref[:, h * DH : (h + 1) * DH] = grad_out
-        gated = (head(query_ref, h).astype(F32) * t.inward(h)).astype(BF16)
-        grad_state_ref[h * DH : (h + 1) * DH, :] = dot(gated, grad_out, ((0,), (0,)))
+        grad_state_ref[h * DH : (h + 1) * DH, :] = dot(
+            head(gated_ref, h), grad_out, ((0,), (0,))
+        )
 
 
 def edge_kernel(outgoing_ref, grad_state_ref, factor_ref, before_ref):
@@ -208,38 +214,60 @@
 
 def intra_kernel(
     start_ref,
-    query_ref,
     key_ref,
     value_ref,
+    gain_ref,
     decay_ref,
     doc_ref,
     grad_out_ref,
-    attend_ref,
     state_ref,
+    output_ref,
+    sums_ref,
+    normed_ref,
     query_grad_ref,
-    key_part_ref,
-    value_part_ref,
 ):
     t = Tables(decay_ref, doc_ref, start_ref)
+    inverse, _ = scales(sums_ref)
     for h in range(t.heads):
+        normed_ref[:, h * DH : (h + 1) * DH] = (
+            head(output_ref, h) * inverse * head(gain_ref, h)
+        ).astype(BF16)
         grad_out = head(grad_out_ref, h)
         mixing = dot(grad_out, head(value_ref, h), ((1,), (1,))) * t.decay(h)
         mixing = mixing.astype(BF16)
         carried = dot(twice(grad_out), state(state_ref, h), ((1,), (1,)))
         query_grad = dot(mixing, head(key_ref, h), ((1,), (0,))) + t.inward(h) * carried
         query_grad_ref[:, h * DH : (h + 1) * DH] = query_grad.astype(BF16)
+
+
+def part_kernel(
+    start_ref,
+    query_ref,
+    value_ref,
+    decay_ref,
+    doc_ref,
+    grad_out_ref,
+    attend_ref,
+    key_part_ref,
+    value_part_ref,
+    outward_ref,
+):
+    t = Tables(decay_ref, doc_ref, start_ref)
+    for h in range(t.heads):
+        grad_out = head(grad_out_ref, h)
+        mixing = dot(grad_out, head(value_ref, h), ((1,), (1,))) * t.decay(h)
+        mixing = mixing.astype(BF16)
         key_part_ref[:, h * DH : (h + 1) * DH] = dot(mixing, head(query_ref, h), ((0,), (0,)))
         value_part_ref[:, h * DH : (h + 1) * DH] = dot(
             state(attend_ref, h), grad_out, ((0,), (0,))
         )
+        outward_ref[h * DH : (h + 1) * DH, :] = t.outward(h)
 
 
 def final_kernel(
-    start_ref,
     key_ref,
     value_ref,
-    decay_ref,
-    doc_ref,
+    outward_ref,
     key_part_ref,
     value_part_ref,
     outgoing_ref,
@@ -247,10 +275,9 @@
     key_grad_ref,
     value_grad_ref,
 ):
-    t = Tables(decay_ref, doc_ref, start_ref)
-    for h in range(t.heads):
+    for h in range(key_ref.shape[1] // DH):
         high, low = split(state(outgoing_ref, h) + state(edge_ref, h))
-        outward = t.outward(h)
+        outward = state(outward_ref, h)
         key_grad = head(key_part_ref, h) + outward * dot(
             twice(head(value_ref, h)), jnp.concatenate([high, low], axis=1), ((1,), (1,))
         )
@@ -261,9 +288,13 @@
         value_grad_ref[:, h * DH : (h + 1) * DH] = value_grad.astype(BF16)
 
 
-def call(kernel, outs, *args, scalars=0):
+def call(kernel, outs, *args, scalars=0, pinned=True):
     vmem = pl.BlockSpec(memory_space=pltpu.VMEM)
     smem = pl.BlockSpec(memory_space=pltpu.SMEM)
+    if pinned:
+        args = args[:scalars] + tuple(
+            pltpu.with_memory_space_constraint(x, pltpu.VMEM) for x in args[scalars:]
+        )
     return pl.pallas_call(
         kernel,
         out_shape=tuple(
@@ -273,7 +304,7 @@
         in_specs=[smem] * scalars + [vmem] * (len(args) - scalars),
         out_specs=(vmem,) * len(outs),
         name=kernel.__name__,
-    )(*args[:scalars], *(pltpu.with_memory_space_constraint(x, pltpu.VMEM) for x in args[scalars:]))
+    )(*args)
 
 
 def exchange(rows, per_block):
@@ -292,88 +323,99 @@
     gains = norm_gain.reshape(1, width)
     states = ((heads * DH, DH), F32, True)
     wide = ((tokens, width), F32, True)
-    narrow = ((tokens, width), BF16)
+    narrow = ((tokens, width), BF16, True)
+    pieces = ((HALF * SUB, DH), F32, True)
     decays = (log_decay, docs)
 
     local, factor = call(
-        local_kernel, (states, ((heads, DH), F32, True)), start, key_rows, value_rows, *decays, scalars=1
+        local_kernel,
+        (states, ((heads, DH), F32, True)),
+        start,
+        key_rows,
+        value_rows,
+        *decays,
+        scalars=1,
+        pinned=False,
     )
     edge = lax.ppermute(local, "ctx", [(HALF - 1, HALF)])
-    attend, inner = call(
+    attend, inner, inward, gated, scaled = call(
         inner_kernel,
-        (((heads * DH, DH), BF16, True), wide),
+        (((heads * DH, DH), BF16, True), wide, states, narrow, wide),
         start,
         queries,
         key_rows,
         value_rows,
+        out_grad,
+        gains,
         *decays,
         scalars=1,
     )
     (packed,) = call(pack_kernel, (((HALF * (SUB + 1), DH), F32, True),), local, factor, edge)
     packed = exchange(packed, SUB + 1)
-    incoming, factors = call(
-        forward_kernel, (((HALF * SUB, DH), F32, True), ((HALF * SUB, DH), F32, True)), packed
-    )
+    incoming, factors = call(forward_kernel, (pieces, pieces), packed)
     incoming = exchange(incoming, SUB)
 
     peers = lax.axis_size("head")
     output, inbound, sums = call(
         output_kernel,
         (wide, ((heads * DH, 2 * DH), BF16, True), ((peers * SUB, DH), F32, True)),
-        start,
         queries,
-        out_grad,
-        gains,
-        *decays,
+        scaled,
+        inward,
         inner,
         incoming,
         edge,
+    )
+    sums = lax.all_to_all(sums.reshape(peers, SUB, DH), "head", 0, 0, tiled=True)
+    sums = sums.reshape(peers * SUB, DH)
+    grad_out, grad_state = call(
+        grad_kernel, (narrow, states), scaled, gated, output, sums
+    )
+
+    arrived = exchange(grad_state, SUB)
+    normed, query_grad = call(
+        intra_kernel,
+        (narrow[:2], narrow[:2]),
+        start,
+        key_rows,
+        value_rows,
+        gains,
+        *decays,
+        grad_out,
+        inbound,
+        output,
+        sums,
         scalars=1,
     )
-    sums = lax.all_to_all(sums.reshape(peers, SUB, DH), "head", 0, 0, tiled=True)
-    normed, grad_out, grad_state = call(
-        grad_kernel,
-        (narrow, (*narrow, True), states),
+    arrived, normed, query_grad = lax.optimization_barrier((arrived, normed, query_grad))
+    (outgoing,) = call(backward_kernel, (pieces,), arrived, factors)
+    outgoing = exchange(outgoing, SUB)
+    key_part, value_part, outward = call(
+        part_kernel,
+        (wide, wide, states),
         start,
         queries,
-        out_grad,
-        gains,
-        *decays,
-        output,
-        sums.reshape(peers * SUB, DH),
-        scalars=1,
-    )
-
-    arrived = exchange(grad_state, SUB)
-    (outgoing,) = call(backward_kernel, (((HALF * SUB, DH), F32, True),), arrived, factors)
-    outgoing = exchange(outgoing, SUB)
-    (before,) = call(edge_kernel, (states,), outgoing, grad_state, factor)
-    after = lax.ppermute(before, "ctx", [(HALF, HALF - 1)])
-    query_grad, key_part, value_part = call(
-        intra_kernel,
-        (narrow, wide, wide),
-        start,
-        queries,
-        key_rows,
         value_rows,
         *decays,
         grad_out,
         attend,
-        inbound,
         scalars=1,
     )
+    outgoing, key_part, value_part, outward = lax.optimization_barrier(
+        (outgoing, key_part, value_part, outward)
+    )
+    (before,) = call(edge_kernel, (states,), outgoing, grad_state, factor)
+    after = lax.ppermute(before, "ctx", [(HALF, HALF - 1)])
     key_grad, value_grad = call(
         final_kernel,
-        (narrow, narrow),
-        start,
+        (narrow[:2], narrow[:2]),
         key_rows,
         value_rows,
-        *decays,
+        outward,
         key_part,
         value_part,
         outgoing,
         after,
-        scalars=1,
     )
     return normed, query_grad, key_grad, value_grad
 

time: 115 us -> 113 us (0.983)
  blocking collectives: 85.1 us -> 48.7 us
  waiting for transfers between devices: 11.2 us -> 32.4 us
  starting transfers between devices: 7 us -> 19.3 us
  Pallas kernels: 7.48 us -> 10.4 us
  local copies, waits for them, and re-layouts: 3.17 us -> 0.61 us
    all_to_all x3 -> x1, blocking collectives: 71.9 us -> 35.6 us  [exchange(): lax.all_to_all(rows.reshape(shape), 'ctx', 0, 0, axis_index_groups=GROUPS...]
    all_to_all x1 -> x3, waiting for transfers between devices: 11.2 us -> 32.4 us  [exchange(): lax.all_to_all(rows.reshape(shape), 'ctx', 0, 0, axis_index_groups=GROUPS...]
    all_to_all x1 -> x3, starting transfers between devices: 5.64 us -> 18 us  [exchange(): lax.all_to_all(rows.reshape(shape), 'ctx', 0, 0, axis_index_groups=GROUPS...]
    pallas_call x10 -> x11, Pallas kernels: 7.48 us -> 10.4 us  [call(): pl.pallas_call(kernel, out_shape=tuple((pltpu.VMEM(shape, kind) if keep e...]
    unnamed x18 -> x14, local copies, waits for them, and re-layouts: 3.17 us -> 0.61 us
  transfers between devices with their start and end apart: 3 -> 5, of which waited for: 1 -> 3; matrix products, arithmetic and copies ran while one was open for 0% -> 0% of each run, Pallas kernels for 2% -> 3%
where the time goes in v3:
time: 113 us; the launch traced here: 112 us
  blocking collectives  48.7 us (43%)
  waiting for transfers between devices  32.4 us (29%)
  starting transfers between devices  19.3 us (17%)
  Pallas kernels  10.4 us (9%)
    all_to_all x1, blocking collectives, exchange(): lax.all_to_all(rows.reshape(shape), 'ctx', 0, 0, axis_index_groups=GROUPS...  35.6 us
    all_to_all x3, waiting for transfers between devices, exchange(): lax.all_to_all(rows.reshape(shape), 'ctx', 0, 0, axis_index_groups=GROUPS...  32.4 us
    all_to_all x3, starting transfers between devices, exchange(): lax.all_to_all(rows.reshape(shape), 'ctx', 0, 0, axis_index_groups=GROUPS...  18 us
    all_to_all x1, blocking collectives, on_device(): lax.all_to_all(sums.reshape(peers, SUB, DH), 'head', 0, 0, tiled=True)  13.2 us
    pallas_call x11, Pallas kernels, call(): pl.pallas_call(kernel, out_shape=tuple((pltpu.VMEM(shape, kind) if keep e...  10.4 us
  transfers between devices with their start and end apart: 5, of which 3 were waited for; matrix products, arithmetic and copies ran while one was open for 0% of the time, Pallas kernels for 3%

profile of v3, /device:TPU:1, one launch (start us, length us, event | category | flops | bytes accessed | tf_op | source)
XLA Modules:
  0.0 112.3 jit_solution(1652339854052025203)
XLA Ops:
  0.6 1.6 %local_kernel.1 = (f32[512,128]{1,0:T(8,128)S(1)}, f32[4,128]{1,0:T(4,128)S(1)}) custom-call(s32[1]{0:T(128)} %bitcast.start_ref, bf16[128,512]{1,0:T(8,128)(2,1)} %key_ref.7, bf16[128,512]{1,0:T(8,128)(2,1)} %value_ref.9, f32[4,128]{1,0:T(4,128)} %decay_ref.7, s32[1,128]{1,0:T(1,128)} %bitcast.24), custom_call_target="tpu_custom_call" | custom-call | tf_op jit(solution)/shard_map/local_kernel/pallas_call | solution.py:298
  2.2 0.7 collective-permute-start
  2.9 0.0 collective-permute-done.edge_ref
  3.0 35.6 %all_to_all.25 = f32[64,9,1,128]{3,2,1,0:T(1,128)S(1)} all-to-all(f32[64,9,1,128]{3,2,1,0:T(1,128)S(1)} %bitcast.15), channel_id=1, replica_groups={{0,8,16,24,32,40,48,56,64,72,80,88,96,104,112,120,128,136,144,152,160,1..., dimensions={0} | all-to-all | bytes 589824 | tf_op jit(solution)/shard_map/all_to_all | solution.py:312
  38.5 0.0 copy-start.4
  38.5 0.0 copy-start.5
  38.5 0.8 forward_kernel.1
  39.4 0.0 copy-start
  39.4 0.0 copy-start.1
  39.4 0.0 copy-start.2
  39.4 0.0 copy-start.3
  39.4 5.7 %all-to-all-start.1 = ((f32[64,8,128]{2,1,0:T(8,128)}), f32[64,8,128]{2,1,0:T(8,128)S(1)}, u32[]{:S(2)}, u32[]{:S(2)}) async-start(f32[64,8,128]{2,1,0:T(8,128)} %bitcast.5), calls=%async_computation.1 | async-start | bytes 524288 | tf_op jit(solution)/shard_map/all_to_all | solution.py:312
  45.0 0.0 copy-start.6
  45.1 0.0 copy-done.4
  45.1 0.0 copy-done.5
  45.1 0.0 copy-done
  45.1 0.0 copy-done.1
  45.1 0.0 copy-done.2
  45.1 0.0 copy-done.3
  45.1 0.6 copy-done.6
  45.7 1.0 inner_kernel.1
  46.7 10.6 %all-to-all-done.1 = f32[64,8,128]{2,1,0:T(8,128)S(1)} async-done(((f32[64,8,128]{2,1,0:T(8,128)}), f32[64,8,128]{2,1,0:T(8,128)S(1)}, u32[]{:S(2)}, u32[]{:S(2)}) %all-to-all-start.1) | async-done | bytes 262176 | tf_op jit(solution)/shard_map/all_to_all | solution.py:312
  57.3 0.5 output_kernel.1
  57.8 13.2 %all_to_all.26 = f32[8,8,128]{2,1,0:T(8,128)S(1)} all-to-all(f32[8,8,128]{2,1,0:T(8,128)S(1)} %bitcast.21), channel_id=1, replica_groups=mesh['ctx'=128,'head'=8] {'head'}, dimensions={0} | all-to-all | bytes 65536 | tf_op jit(solution)/shard_map/all_to_all | solution.py:369
  71.0 1.0 grad_kernel.1
  71.9 6.9 %all-to-all-start.3 = ((f32[64,8,128]{2,1,0:T(8,128)}), f32[64,8,128]{2,1,0:T(8,128)S(1)}, u32[]{:S(2)}, u32[]{:S(2)}) async-start(f32[64,8,128]{2,1,0:T(8,128)} %bitcast.9), calls=%async_computation.3 | async-start | bytes 524288 | tf_op jit(solution)/shard_map/all_to_all | solution.py:312
  78.8 1.5 %intra_kernel.1 = (bf16[128,512]{1,0:T(8,128)(2,1)}, bf16[128,512]{1,0:T(8,128)(2,1)}) custom-call(s32[1]{0:T(128)} %bitcast.start_ref, bf16[128,512]{1,0:T(8,128)(2,1)S(1)} %copy-done.1, bf16[128,512]{1,0:T(8,128)(2,1)S(1)} %copy-done, f32[1,512]{1,0:T(1,128)S(1)} %bitcast.23, f32[4,128]{1,0:T(4,128)S(1)} %copy-done.4, s32[1,128]{1,0:T(1,128)S(1)} %bitcast.26, ...), custom_call_target="tpu_custom_call" | custom-call | tf_op jit(solution)/shard_map/intra_kernel/pallas_call | solution.py:298
  80.4 10.7 %all-to-all-done.3 = f32[64,8,128]{2,1,0:T(8,128)S(1)} async-done(((f32[64,8,128]{2,1,0:T(8,128)}), f32[64,8,128]{2,1,0:T(8,128)S(1)}, u32[]{:S(2)}, u32[]{:S(2)}) %all-to-all-start.3) | async-done | bytes 262176 | tf_op jit(solution)/shard_map/all_to_all | solution.py:312
  91.1 0.8 backward_kernel.1
  91.9 5.5 %all-to-all-start.4 = ((f32[64,8,128]{2,1,0:T(8,128)}), f32[64,8,128]{2,1,0:T(8,128)S(1)}, u32[]{:S(2)}, u32[]{:S(2)}) async-start(f32[64,8,128]{2,1,0:T(8,128)} %bitcast.11), calls=%async_computation.4 | async-start | bytes 524288 | tf_op jit(solution)/shard_map/all_to_all | solution.py:312
  97.4 1.1 %part_kernel.1 = (f32[128,512]{1,0:T(8,128)S(1)}, f32[128,512]{1,0:T(8,128)S(1)}, f32[512,128]{1,0:T(8,128)S(1)}) custom-call(s32[1]{0:T(128)} %bitcast.start_ref, bf16[128,512]{1,0:T(8,128)(2,1)S(1)} %copy-done.2, bf16[128,512]{1,0:T(8,128)(2,1)S(1)} %copy-done, f32[4,128]{1,0:T(4,128)S(1)} %copy-done.4, s32[1,128]{1,0:T(1,128)S(1)} %bitcast.27, ...), custom_call_target="tpu_custom_call" | custom-call | tf_op jit(solution)/shard_map/part_kernel/pallas_call | solution.py:298
  98.5 11.1 %all-to-all-done.4 = f32[64,8,128]{2,1,0:T(8,128)S(1)} async-done(((f32[64,8,128]{2,1,0:T(8,128)}), f32[64,8,128]{2,1,0:T(8,128)S(1)}, u32[]{:S(2)}, u32[]{:S(2)}) %all-to-all-start.4) | async-done | bytes 262176 | tf_op jit(solution)/shard_map/all_to_all | solution.py:312
  109.6 1.0 edge_kernel.1
  110.6 0.7 collective-permute-start.1
  111.3 0.0 collective-permute-done.1.edge_ref
  111.3 1.0 final_kernel.1
  (1 shorter events, 0.0 us)
Async XLA Ops:
  2.2 0.7 collective-permute-start
  38.5 6.5 %copy-start.4 = (f32[4,128]{1,0:T(4,128)S(1)}, f32[4,128]{1,0:T(4,128)}, u32[]{:S(2)}) copy-start(f32[4,128]{1,0:T(4,128)} %decay_ref.7) | copy-start | bytes 6148
  38.5 6.5 %copy-start.5 = (f32[512]{0:T(512)S(1)}, f32[512]{0:T(512)}, u32[]{:S(2)}) copy-start(f32[512]{0:T(512)} %param.13) | copy-start | bytes 6148
  39.4 5.7 %copy-start = (bf16[128,512]{1,0:T(8,128)(2,1)S(1)}, bf16[128,512]{1,0:T(8,128)(2,1)}, u32[]{:S(2)}) copy-start(bf16[128,512]{1,0:T(8,128)(2,1)} %value_ref.9) | copy-start | bytes 393220
  39.4 5.7 %copy-start.1 = (bf16[128,512]{1,0:T(8,128)(2,1)S(1)}, bf16[128,512]{1,0:T(8,128)(2,1)}, u32[]{:S(2)}) copy-start(bf16[128,512]{1,0:T(8,128)(2,1)} %key_ref.7) | copy-start | bytes 393220
  39.4 5.7 %copy-start.2 = (bf16[128,512]{1,0:T(8,128)(2,1)S(1)}, bf16[128,512]{1,0:T(8,128)(2,1)}, u32[]{:S(2)}) copy-start(bf16[128,512]{1,0:T(8,128)(2,1)} %query_ref.5) | copy-start | bytes 393220
  39.4 5.7 %copy-start.3 = (bf16[128,512]{1,0:T(8,128)(2,1)S(1)}, bf16[128,512]{1,0:T(8,128)(2,1)}, u32[]{:S(2)}) copy-start(bf16[128,512]{1,0:T(8,128)(2,1)} %grad_ref.1) | copy-start | bytes 393220
  39.4 17.9 %all-to-all-start.1 = ((f32[64,8,128]{2,1,0:T(8,128)}), f32[64,8,128]{2,1,0:T(8,128)S(1)}, u32[]{:S(2)}, u32[]{:S(2)}) async-start(f32[64,8,128]{2,1,0:T(8,128)} %bitcast.5), calls=%async_computation.1 | async-start | bytes 524288 | tf_op jit(solution)/shard_map/all_to_all | solution.py:312
  45.0 0.7 copy-start.6
  71.9 19.1 %all-to-all-start.3 = ((f32[64,8,128]{2,1,0:T(8,128)}), f32[64,8,128]{2,1,0:T(8,128)S(1)}, u32[]{:S(2)}, u32[]{:S(2)}) async-start(f32[64,8,128]{2,1,0:T(8,128)} %bitcast.9), calls=%async_computation.3 | async-start | bytes 524288 | tf_op jit(solution)/shard_map/all_to_all | solution.py:312
  91.9 17.7 %all-to-all-start.4 = ((f32[64,8,128]{2,1,0:T(8,128)}), f32[64,8,128]{2,1,0:T(8,128)S(1)}, u32[]{:S(2)}, u32[]{:S(2)}) async-start(f32[64,8,128]{2,1,0:T(8,128)} %bitcast.11), calls=%async_computation.4 | async-start | bytes 524288 | tf_op jit(solution)/shard_map/all_to_all | solution.py:312
  110.6 0.7 collective-permute-start.1

commit v4 on v3

--- a/solution.py
+++ b/solution.py
@@ -80,6 +80,32 @@
 
 def state(ref, h):
     return ref[h * DH : (h + 1) * DH, :]
+
+
+def source_kernel(start_ref, key_hbm, value_hbm, decay_hbm, doc_hbm, local_ref, *scratch):
+    key_ref, value_ref, decay_ref, doc_ref, sems = scratch
+
+    @pl.when(start_ref[0] == (HALF - 1) * key_hbm.shape[0])
+    def _():
+        copies = [
+            pltpu.make_async_copy(src, dst, sems.at[i])
+            for i, (src, dst) in enumerate(
+                (
+                    (decay_hbm, decay_ref),
+                    (doc_hbm, doc_ref),
+                    (key_hbm, key_ref),
+                    (value_hbm, value_ref),
+                )
+            )
+        ]
+        for copy in copies:
+            copy.start()
+        for copy in copies:
+            copy.wait()
+        t = Tables(decay_ref, doc_ref, start_ref)
+        for h in range(t.heads):
+            weighted = (head(key_ref, h).astype(F32) * t.outward(h)).astype(BF16)
+            local_ref[h * DH : (h + 1) * DH, :] = dot(weighted, head(value_ref, h), ((0,), (0,)))
 
 
 def local_kernel(start_ref, key_ref, value_ref, decay_ref, doc_ref, local_ref, factor_ref):
@@ -248,9 +274,11 @@
     doc_ref,
     grad_out_ref,
     attend_ref,
+    grad_state_ref,
     key_part_ref,
     value_part_ref,
     outward_ref,
+    own_ref,
 ):
     t = Tables(decay_ref, doc_ref, start_ref)
     for h in range(t.heads):
@@ -262,6 +290,7 @@
             state(attend_ref, h), grad_out, ((0,), (0,))
         )
         outward_ref[h * DH : (h + 1) * DH, :] = t.outward(h)
+        own_ref[h * DH : (h + 1) * DH, :] = state(grad_state_ref, h)
 
 
 def final_kernel(
@@ -327,6 +356,18 @@
     pieces = ((HALF * SUB, DH), F32, True)
     decays = (log_decay, docs)
 
+    source = pl.pallas_call(
+        source_kernel,
+        out_shape=pltpu.VMEM(*states[:2]),
+        in_specs=[pl.BlockSpec(memory_space=pltpu.SMEM)] + [pl.BlockSpec(memory_space=pl.ANY)] * 4,
+        out_specs=pl.BlockSpec(memory_space=pltpu.VMEM),
+        scratch_shapes=[
+            pltpu.VMEM(x.shape, x.dtype) for x in (key_rows, value_rows, *decays)
+        ]
+        + [pltpu.SemaphoreType.DMA((4,))],
+        name="source_kernel",
+    )(start, key_rows, value_rows, *decays)
+    edge = lax.ppermute(source, "ctx", [(HALF - 1, HALF)])
     local, factor = call(
         local_kernel,
         (states, ((heads, DH), F32, True)),
@@ -337,7 +378,6 @@
         scalars=1,
         pinned=False,
     )
-    edge = lax.ppermute(local, "ctx", [(HALF - 1, HALF)])
     attend, inner, inward, gated, scaled = call(
         inner_kernel,
         (((heads * DH, DH), BF16, True), wide, states, narrow, wide),
@@ -390,21 +430,22 @@
     arrived, normed, query_grad = lax.optimization_barrier((arrived, normed, query_grad))
     (outgoing,) = call(backward_kernel, (pieces,), arrived, factors)
     outgoing = exchange(outgoing, SUB)
-    key_part, value_part, outward = call(
+    key_part, value_part, outward, own = call(
         part_kernel,
-        (wide, wide, states),
+        (wide, wide, states, states),
         start,
         queries,
         value_rows,
         *decays,
         grad_out,
         attend,
+        grad_state,
         scalars=1,
     )
-    outgoing, key_part, value_part, outward = lax.optimization_barrier(
-        (outgoing, key_part, value_part, outward)
-    )
-    (before,) = call(edge_kernel, (states,), outgoing, grad_state, factor)
+    outgoing, key_part, value_part, outward, own = lax.optimization_barrier(
+        (outgoing, key_part, value_part, outward, own)
+    )
+    (before,) = call(edge_kernel, (states,), outgoing, own, factor)
     after = lax.ppermute(before, "ctx", [(HALF, HALF - 1)])
     key_grad, value_grad = call(
         final_kernel,

time: 113 us -> 111 us (0.982)
  blocking collectives: 48.7 us -> 47.1 us
    all_to_all x1, blocking collectives: 35.6 us -> 33.9 us  [exchange(): lax.all_to_all(rows.reshape(shape), 'ctx', 0, 0, axis_index_groups=GROUPS...]
  transfers between devices with their start and end apart: 5 -> 5, of which waited for: 3 -> 3; matrix products, arithmetic and copies ran while one was open for 0% -> 0% of each run, Pallas kernels for 3% -> 6%
where the time goes in v4:
time: 111 us; the launch traced here: 110 us
  blocking collectives  47.1 us (42%)
  waiting for transfers between devices  31.4 us (28%)
  starting transfers between devices  19.3 us (17%)
  Pallas kernels  10.5 us (9%)
    all_to_all x1, blocking collectives, exchange(): lax.all_to_all(rows.reshape(shape), 'ctx', 0, 0, axis_index_groups=GROUPS...  33.9 us
    all_to_all x3, waiting for transfers between devices, exchange(): lax.all_to_all(rows.reshape(shape), 'ctx', 0, 0, axis_index_groups=GROUPS...  31.4 us
    all_to_all x3, starting transfers between devices, exchange(): lax.all_to_all(rows.reshape(shape), 'ctx', 0, 0, axis_index_groups=GROUPS...  18 us
    all_to_all x1, blocking collectives, on_device(): lax.all_to_all(sums.reshape(peers, SUB, DH), 'head', 0, 0, tiled=True)  13.2 us
    pallas_call x11, Pallas kernels, call(): pl.pallas_call(kernel, out_shape=tuple((pltpu.VMEM(shape, kind) if keep e...  10.5 us
  transfers between devices with their start and end apart: 5, of which 3 were waited for; matrix products, arithmetic and copies ran while one was open for 0% of the time, Pallas kernels for 6%

profile of v4, /device:TPU:1, one launch (start us, length us, event | category | flops | bytes accessed | tf_op | source)
XLA Modules:
  0.0 109.8 jit_solution(10395008874865913197)
XLA Ops:
  0.7 0.7 collective-permute-start
  1.4 1.6 %local_kernel.1 = (f32[512,128]{1,0:T(8,128)S(1)}, f32[4,128]{1,0:T(4,128)S(1)}) custom-call(s32[1]{0:T(128)} %bitcast.start_ref, bf16[128,512]{1,0:T(8,128)(2,1)} %key_ref.7, bf16[128,512]{1,0:T(8,128)(2,1)} %value_ref.9, f32[4,128]{1,0:T(4,128)} %decay_ref.7, s32[1,128]{1,0:T(1,128)} %bitcast.23), custom_call_target="tpu_custom_call" | custom-call | tf_op jit(solution)/shard_map/local_kernel/pallas_call | solution.py:327
  3.0 0.0 collective-permute-done.edge_ref
  3.0 33.9 %all_to_all.25 = f32[64,9,1,128]{3,2,1,0:T(1,128)S(1)} all-to-all(f32[64,9,1,128]{3,2,1,0:T(1,128)S(1)} %bitcast.15), channel_id=1, replica_groups={{0,8,16,24,32,40,48,56,64,72,80,88,96,104,112,120,128,136,144,152,160,1..., dimensions={0} | all-to-all | bytes 589824 | tf_op jit(solution)/shard_map/all_to_all | solution.py:341
  37.0 0.0 copy-start.4
  37.0 0.0 copy-start.6
  37.0 0.8 forward_kernel.1
  37.8 0.0 copy-start
  37.8 0.0 copy-start.1
  37.8 0.0 copy-start.2
  37.8 0.0 copy-start.3
  37.8 5.7 %all-to-all-start.1 = ((f32[64,8,128]{2,1,0:T(8,128)}), f32[64,8,128]{2,1,0:T(8,128)S(1)}, u32[]{:S(2)}, u32[]{:S(2)}) async-start(f32[64,8,128]{2,1,0:T(8,128)} %bitcast.5), calls=%async_computation.1 | async-start | bytes 524288 | tf_op jit(solution)/shard_map/all_to_all | solution.py:341
  43.5 0.0 copy-start.5
  43.5 0.0 copy-done.4
  43.5 0.0 copy-done.6
  43.5 0.0 copy-done
  43.5 0.0 copy-done.1
  43.5 0.0 copy-done.2
  43.6 0.0 copy-done.3
  43.6 0.6 copy-done.5
  44.1 1.0 inner_kernel.1
  45.1 10.6 %all-to-all-done.1 = f32[64,8,128]{2,1,0:T(8,128)S(1)} async-done(((f32[64,8,128]{2,1,0:T(8,128)}), f32[64,8,128]{2,1,0:T(8,128)S(1)}, u32[]{:S(2)}, u32[]{:S(2)}) %all-to-all-start.1) | async-done | bytes 262176 | tf_op jit(solution)/shard_map/all_to_all | solution.py:341
  55.7 0.5 output_kernel.1
  56.3 13.2 %all_to_all.26 = f32[8,8,128]{2,1,0:T(8,128)S(1)} all-to-all(f32[8,8,128]{2,1,0:T(8,128)S(1)} %bitcast.21), channel_id=1, replica_groups=mesh['ctx'=128,'head'=8] {'head'}, dimensions={0} | all-to-all | bytes 65536 | tf_op jit(solution)/shard_map/all_to_all | solution.py:409
  69.4 1.0 grad_kernel.1
  70.4 6.9 %all-to-all-start.3 = ((f32[64,8,128]{2,1,0:T(8,128)}), f32[64,8,128]{2,1,0:T(8,128)S(1)}, u32[]{:S(2)}, u32[]{:S(2)}) async-start(f32[64,8,128]{2,1,0:T(8,128)} %bitcast.9), calls=%async_computation.3 | async-start | bytes 524288 | tf_op jit(solution)/shard_map/all_to_all | solution.py:341
  77.3 1.5 %intra_kernel.1 = (bf16[128,512]{1,0:T(8,128)(2,1)}, bf16[128,512]{1,0:T(8,128)(2,1)}) custom-call(s32[1]{0:T(128)} %bitcast.start_ref, bf16[128,512]{1,0:T(8,128)(2,1)S(1)} %copy-done.1, bf16[128,512]{1,0:T(8,128)(2,1)S(1)} %copy-done, f32[1,512]{1,0:T(1,128)S(1)} %bitcast.28, f32[4,128]{1,0:T(4,128)S(1)} %copy-done.4, s32[1,128]{1,0:T(1,128)S(1)} %bitcast.25, ...), custom_call_target="tpu_custom_call" | custom-call | tf_op jit(solution)/shard_map/intra_kernel/pallas_call | solution.py:327
  78.8 10.7 %all-to-all-done.3 = f32[64,8,128]{2,1,0:T(8,128)S(1)} async-done(((f32[64,8,128]{2,1,0:T(8,128)}), f32[64,8,128]{2,1,0:T(8,128)S(1)}, u32[]{:S(2)}, u32[]{:S(2)}) %all-to-all-start.3) | async-done | bytes 262176 | tf_op jit(solution)/shard_map/all_to_all | solution.py:341
  89.5 0.8 backward_kernel.1
  90.4 5.5 %all-to-all-start.4 = ((f32[64,8,128]{2,1,0:T(8,128)}), f32[64,8,128]{2,1,0:T(8,128)S(1)}, u32[]{:S(2)}, u32[]{:S(2)}) async-start(f32[64,8,128]{2,1,0:T(8,128)} %bitcast.11), calls=%async_computation.4 | async-start | bytes 524288 | tf_op jit(solution)/shard_map/all_to_all | solution.py:341
  95.8 2.1 %part_kernel.1 = (f32[128,512]{1,0:T(8,128)S(1)}, f32[128,512]{1,0:T(8,128)S(1)}, f32[512,128]{1,0:T(8,128)S(1)}, f32[512,128]{1,0:T(8,128)S(1)}) custom-call(s32[1]{0:T(128)} %bitcast.start_ref, bf16[128,512]{1,0:T(8,128)(2,1)S(1)} %copy-done.2, bf16[128,512]{1,0:T(8,128)(2,1)S(1)} %copy-done, f32[4,128]{1,0:T(4,128)S(1)} %copy-done.4, ...), custom_call_target="tpu_custom_call" | custom-call | tf_op jit(solution)/shard_map/part_kernel/pallas_call | solution.py:327
  97.9 10.2 %all-to-all-done.4 = f32[64,8,128]{2,1,0:T(8,128)S(1)} async-done(((f32[64,8,128]{2,1,0:T(8,128)}), f32[64,8,128]{2,1,0:T(8,128)S(1)}, u32[]{:S(2)}, u32[]{:S(2)}) %all-to-all-start.4) | async-done | bytes 262176 | tf_op jit(solution)/shard_map/all_to_all | solution.py:341
  108.1 0.7 collective-permute-start.1
  108.8 0.0 collective-permute-done.1.edge_ref
  108.8 1.0 final_kernel.1
  (3 shorter events, 0.1 us)
Async XLA Ops:
  0.7 2.3 %collective-permute-start = (f32[512,128]{1,0:T(8,128)S(1)}, f32[512,128]{1,0:T(8,128)S(1)}, u32[]{:S(2)}, u32[]{:S(2)}) collective-permute-start(f32[512,128]{1,0:T(8,128)S(1)} %source_kernel.1), channel_id=1, source_target_pairs={{504,512},{505,513},{506,514},{507,515},{508,516},{509,517},{510,5... | collective-permute-start | bytes 786440 | tf_op jit(solution)/shard_map/ppermute | solution.py:370
  37.0 6.5 %copy-start.4 = (f32[4,128]{1,0:T(4,128)S(1)}, f32[4,128]{1,0:T(4,128)}, u32[]{:S(2)}) copy-start(f32[4,128]{1,0:T(4,128)} %decay_ref.7) | copy-start | bytes 6148
  37.0 6.5 %copy-start.6 = (f32[512]{0:T(512)S(1)}, f32[512]{0:T(512)}, u32[]{:S(2)}) copy-start(f32[512]{0:T(512)} %param.13) | copy-start | bytes 6148
  37.8 5.7 %copy-start = (bf16[128,512]{1,0:T(8,128)(2,1)S(1)}, bf16[128,512]{1,0:T(8,128)(2,1)}, u32[]{:S(2)}) copy-start(bf16[128,512]{1,0:T(8,128)(2,1)} %value_ref.9) | copy-start | bytes 393220
  37.8 5.7 %copy-start.1 = (bf16[128,512]{1,0:T(8,128)(2,1)S(1)}, bf16[128,512]{1,0:T(8,128)(2,1)}, u32[]{:S(2)}) copy-start(bf16[128,512]{1,0:T(8,128)(2,1)} %key_ref.7) | copy-start | bytes 393220
  37.8 5.7 %copy-start.2 = (bf16[128,512]{1,0:T(8,128)(2,1)S(1)}, bf16[128,512]{1,0:T(8,128)(2,1)}, u32[]{:S(2)}) copy-start(bf16[128,512]{1,0:T(8,128)(2,1)} %query_ref.5) | copy-start | bytes 393220
  37.8 5.7 %copy-start.3 = (bf16[128,512]{1,0:T(8,128)(2,1)S(1)}, bf16[128,512]{1,0:T(8,128)(2,1)}, u32[]{:S(2)}) copy-start(bf16[128,512]{1,0:T(8,128)(2,1)} %grad_ref.1) | copy-start | bytes 393220
  37.8 17.9 %all-to-all-start.1 = ((f32[64,8,128]{2,1,0:T(8,128)}), f32[64,8,128]{2,1,0:T(8,128)S(1)}, u32[]{:S(2)}, u32[]{:S(2)}) async-start(f32[64,8,128]{2,1,0:T(8,128)} %bitcast.5), calls=%async_computation.1 | async-start | bytes 524288 | tf_op jit(solution)/shard_map/all_to_all | solution.py:341
  43.5 0.7 copy-start.5
  70.4 19.1 %all-to-all-start.3 = ((f32[64,8,128]{2,1,0:T(8,128)}), f32[64,8,128]{2,1,0:T(8,128)S(1)}, u32[]{:S(2)}, u32[]{:S(2)}) async-start(f32[64,8,128]{2,1,0:T(8,128)} %bitcast.9), calls=%async_computation.3 | async-start | bytes 524288 | tf_op jit(solution)/shard_map/all_to_all | solution.py:341
  90.4 17.7 %all-to-all-start.4 = ((f32[64,8,128]{2,1,0:T(8,128)}), f32[64,8,128]{2,1,0:T(8,128)S(1)}, u32[]{:S(2)}, u32[]{:S(2)}) async-start(f32[64,8,128]{2,1,0:T(8,128)} %bitcast.11), calls=%async_computation.4 | async-start | bytes 524288 | tf_op jit(solution)/shard_map/all_to_all | solution.py:341
  108.1 0.7 collective-permute-start.1

commit v5 on v4

--- a/solution.py
+++ b/solution.py
@@ -154,7 +154,26 @@
         packed_ref[at + SUB : at + SUB + 1, :] = factor
 
 
-def forward_kernel(packed_ref, incoming_ref, factor_ref):
+class Outbox:
+    def __init__(self, out, buffer, sems):
+        self.out, self.buffer, self.sems, self.copies = out, buffer, sems, []
+
+    def send(self, part):
+        at = len(self.copies)
+        copy = pltpu.make_async_copy(self.buffer.at[part], self.out.at[part], self.sems.at[at])
+        copy.start()
+        self.copies.append(copy)
+
+    def wait(self):
+        for copy in self.copies:
+            copy.wait()
+
+
+QUARTER = HALF // 4
+
+
+def forward_kernel(packed_ref, incoming_hbm, factor_ref, incoming_ref, sems):
+    outbox = Outbox(incoming_hbm, incoming_ref, sems)
     carry = jnp.zeros((SUB, DH), F32)
     for b in range(HALF):
         at = b * (SUB + 1)
@@ -163,14 +182,21 @@
         incoming_ref[rows, :] = carry
         factor_ref[rows, :] = factor
         carry = factor * carry + packed_ref[at : at + SUB, :]
-
-
-def backward_kernel(grad_ref, factor_ref, outgoing_ref):
+        if b % QUARTER == QUARTER - 1:
+            outbox.send(pl.ds((b + 1 - QUARTER) * SUB, QUARTER * SUB))
+    outbox.wait()
+
+
+def backward_kernel(grad_ref, factor_ref, outgoing_hbm, outgoing_ref, sems):
+    outbox = Outbox(outgoing_hbm, outgoing_ref, sems)
     carry = jnp.zeros((SUB, DH), F32)
     for b in reversed(range(HALF)):
         rows = pl.ds(b * SUB, SUB)
         outgoing_ref[rows, :] = carry
         carry = factor_ref[rows, :] * carry + grad_ref[rows, :]
+        if b % QUARTER == 0:
+            outbox.send(pl.ds(b * SUB, QUARTER * SUB))
+    outbox.wait()
 
 
 def output_kernel(
@@ -220,8 +246,11 @@
     output_ref,
     sums_ref,
     grad_out_ref,
+    grad_state_hbm,
     grad_state_ref,
+    sems,
 ):
+    outbox = Outbox(grad_state_hbm, grad_state_ref, sems)
     inverse, pull = scales(sums_ref)
     for h in range(scaled_ref.shape[1] // DH):
         grad_out = (inverse * head(scaled_ref, h) - head(output_ref, h) * pull).astype(BF16)
@@ -229,6 +258,8 @@
         grad_state_ref[h * DH : (h + 1) * DH, :] = dot(
             head(gated_ref, h), grad_out, ((0,), (0,))
         )
+        outbox.send(pl.ds(h * DH, DH))
+    outbox.wait()
 
 
 def edge_kernel(outgoing_ref, grad_state_ref, factor_ref, before_ref):
@@ -301,9 +332,15 @@
     value_part_ref,
     outgoing_ref,
     edge_ref,
+    key_grad_hbm,
+    value_grad_hbm,
     key_grad_ref,
     value_grad_ref,
+    key_sems,
+    value_sems,
 ):
+    key_box = Outbox(key_grad_hbm, key_grad_ref, key_sems)
+    value_box = Outbox(value_grad_hbm, value_grad_ref, value_sems)
     for h in range(key_ref.shape[1] // DH):
         high, low = split(state(outgoing_ref, h) + state(edge_ref, h))
         outward = state(outward_ref, h)
@@ -315,9 +352,13 @@
         )
         key_grad_ref[:, h * DH : (h + 1) * DH] = key_grad.astype(BF16)
         value_grad_ref[:, h * DH : (h + 1) * DH] = value_grad.astype(BF16)
-
-
-def call(kernel, outs, *args, scalars=0, pinned=True):
+        key_box.send((slice(None), pl.ds(h * DH, DH)))
+        value_box.send((slice(None), pl.ds(h * DH, DH)))
+    key_box.wait()
+    value_box.wait()
+
+
+def call(kernel, outs, *args, scalars=0, pinned=True, boxes=()):
     vmem = pl.BlockSpec(memory_space=pltpu.VMEM)
     smem = pl.BlockSpec(memory_space=pltpu.SMEM)
     if pinned:
@@ -331,7 +372,11 @@
             for shape, kind, *keep in outs
         ),
         in_specs=[smem] * scalars + [vmem] * (len(args) - scalars),
-        out_specs=(vmem,) * len(outs),
+        out_specs=tuple(
+            pl.BlockSpec(memory_space=pl.ANY) if i in boxes else vmem for i in range(len(outs))
+        ),
+        scratch_shapes=[pltpu.VMEM(*outs[i][:2]) for i in boxes]
+        + [pltpu.SemaphoreType.DMA((4,)) for i in boxes],
         name=kernel.__name__,
     )(*args)
 
@@ -392,7 +437,7 @@
     )
     (packed,) = call(pack_kernel, (((HALF * (SUB + 1), DH), F32, True),), local, factor, edge)
     packed = exchange(packed, SUB + 1)
-    incoming, factors = call(forward_kernel, (pieces, pieces), packed)
+    incoming, factors = call(forward_kernel, (pieces[:2], pieces), packed, boxes=(0,))
     incoming = exchange(incoming, SUB)
 
     peers = lax.axis_size("head")
@@ -409,7 +454,7 @@
     sums = lax.all_to_all(sums.reshape(peers, SUB, DH), "head", 0, 0, tiled=True)
     sums = sums.reshape(peers * SUB, DH)
     grad_out, grad_state = call(
-        grad_kernel, (narrow, states), scaled, gated, output, sums
+        grad_kernel, (narrow, states[:2]), scaled, gated, output, sums, boxes=(1,)
     )
 
     arrived = exchange(grad_state, SUB)
@@ -428,7 +473,7 @@
         scalars=1,
     )
     arrived, normed, query_grad = lax.optimization_barrier((arrived, normed, query_grad))
-    (outgoing,) = call(backward_kernel, (pieces,), arrived, factors)
+    (outgoing,) = call(backward_kernel, (pieces[:2],), arrived, factors, boxes=(0,))
     outgoing = exchange(outgoing, SUB)
     key_part, value_part, outward, own = call(
         part_kernel,
@@ -457,6 +502,7 @@
         value_part,
         outgoing,
         after,
+        boxes=(0, 1),
     )
     return normed, query_grad, key_grad, value_grad
 

time: 111 us -> 111 us (level)
  transfers between devices with their start and end apart: 5 -> 5, of which waited for: 3 -> 3; matrix products, arithmetic and copies ran while one was open for 0% -> 0% of each run, Pallas kernels for 6% -> 5%
where the time goes in v5:
time: 111 us; the launch traced here: 110 us
  blocking collectives  47.1 us (42%)
  waiting for transfers between devices  32.4 us (29%)
  starting transfers between devices  19.5 us (18%)
  Pallas kernels  9.48 us (9%)
    all_to_all x1, blocking collectives, exchange(): lax.all_to_all(rows.reshape(shape), 'ctx', 0, 0, axis_index_groups=GROUPS...  33.9 us
    all_to_all x3, waiting for transfers between devices, exchange(): lax.all_to_all(rows.reshape(shape), 'ctx', 0, 0, axis_index_groups=GROUPS...  32.4 us
    all_to_all x3, starting transfers between devices, exchange(): lax.all_to_all(rows.reshape(shape), 'ctx', 0, 0, axis_index_groups=GROUPS...  18.1 us
    all_to_all x1, blocking collectives, on_device(): lax.all_to_all(sums.reshape(peers, SUB, DH), 'head', 0, 0, tiled=True)  13.2 us
    pallas_call x11, Pallas kernels, call(): pl.pallas_call(kernel, out_shape=tuple((pltpu.VMEM(shape, kind) if keep e...  9.44 us
  transfers between devices with their start and end apart: 5, of which 3 were waited for; matrix products, arithmetic and copies ran while one was open for 0% of the time, Pallas kernels for 5%

profile of v5, /device:TPU:1, one launch (start us, length us, event | category | flops | bytes accessed | tf_op | source)
XLA Modules:
  0.0 109.9 jit_solution(794949454412705272)
XLA Ops:
  0.7 0.7 collective-permute-start
  1.4 1.6 %local_kernel.1 = (f32[512,128]{1,0:T(8,128)S(1)}, f32[4,128]{1,0:T(4,128)S(1)}) custom-call(s32[1]{0:T(128)} %bitcast.start_ref, bf16[128,512]{1,0:T(8,128)(2,1)} %key_ref.7, bf16[128,512]{1,0:T(8,128)(2,1)} %value_ref.9, f32[4,128]{1,0:T(4,128)} %decay_ref.7, s32[1,128]{1,0:T(1,128)} %bitcast.24), custom_call_target="tpu_custom_call" | custom-call | tf_op jit(solution)/shard_map/local_kernel/pallas_call | solution.py:368
  3.0 0.0 collective-permute-done.edge_ref
  3.0 33.9 %all_to_all.25 = f32[64,9,1,128]{3,2,1,0:T(1,128)S(1)} all-to-all(f32[64,9,1,128]{3,2,1,0:T(1,128)S(1)} %bitcast.15), channel_id=1, replica_groups={{0,8,16,24,32,40,48,56,64,72,80,88,96,104,112,120,128,136,144,152,160,1..., dimensions={0} | all-to-all | bytes 589824 | tf_op jit(solution)/shard_map/all_to_all | solution.py:386
  37.0 0.0 copy-start.5
  37.0 0.0 copy-start.7
  37.0 0.8 forward_kernel.1
  37.8 0.0 copy-start
  37.8 0.0 copy-start.1
  37.8 0.0 copy-start.2
  37.8 0.0 copy-start.4
  37.8 5.7 %all-to-all-start.1 = ((f32[64,8,128]{2,1,0:T(8,128)}), f32[64,8,128]{2,1,0:T(8,128)S(1)}, u32[]{:S(2)}, u32[]{:S(2)}) async-start(f32[64,8,128]{2,1,0:T(8,128)} %bitcast.31), calls=%async_computation.1 | async-start | bytes 524288 | tf_op jit(solution)/shard_map/all_to_all | solution.py:386
  43.5 0.0 copy-start.6
  43.5 0.0 copy-done.5
  43.5 0.0 copy-done.7
  43.5 0.0 copy-done
  43.5 0.0 copy-done.1
  43.5 0.0 copy-done.2
  43.6 0.0 copy-done.4
  43.6 0.6 copy-done.6
  44.2 1.0 inner_kernel.1
  45.1 10.6 %all-to-all-done.1 = f32[64,8,128]{2,1,0:T(8,128)S(1)} async-done(((f32[64,8,128]{2,1,0:T(8,128)}), f32[64,8,128]{2,1,0:T(8,128)S(1)}, u32[]{:S(2)}, u32[]{:S(2)}) %all-to-all-start.1) | async-done | bytes 262176 | tf_op jit(solution)/shard_map/all_to_all | solution.py:386
  55.7 0.5 output_kernel.1
  56.2 13.2 %all_to_all.26 = f32[8,8,128]{2,1,0:T(8,128)S(1)} all-to-all(f32[8,8,128]{2,1,0:T(8,128)S(1)} %bitcast.22), channel_id=1, replica_groups=mesh['ctx'=128,'head'=8] {'head'}, dimensions={0} | all-to-all | bytes 65536 | tf_op jit(solution)/shard_map/all_to_all | solution.py:454
  69.4 1.0 grad_kernel.1
  70.4 6.9 %all-to-all-start.3 = ((f32[64,8,128]{2,1,0:T(8,128)}), f32[64,8,128]{2,1,0:T(8,128)S(1)}, u32[]{:S(2)}, u32[]{:S(2)}) async-start(f32[64,8,128]{2,1,0:T(8,128)} %bitcast.18), calls=%async_computation.3 | async-start | bytes 524288 | tf_op jit(solution)/shard_map/all_to_all | solution.py:386
  77.3 1.5 %intra_kernel.1 = (bf16[128,512]{1,0:T(8,128)(2,1)}, bf16[128,512]{1,0:T(8,128)(2,1)}) custom-call(s32[1]{0:T(128)} %bitcast.start_ref, bf16[128,512]{1,0:T(8,128)(2,1)S(1)} %copy-done.1, bf16[128,512]{1,0:T(8,128)(2,1)S(1)} %copy-done, f32[1,512]{1,0:T(1,128)S(1)} %bitcast.29, f32[4,128]{1,0:T(4,128)S(1)} %copy-done.5, s32[1,128]{1,0:T(1,128)S(1)} %bitcast.26, ...), custom_call_target="tpu_custom_call" | custom-call | tf_op jit(solution)/shard_map/intra_kernel/pallas_call | solution.py:368
  78.9 10.7 %all-to-all-done.3 = f32[64,8,128]{2,1,0:T(8,128)S(1)} async-done(((f32[64,8,128]{2,1,0:T(8,128)}), f32[64,8,128]{2,1,0:T(8,128)S(1)}, u32[]{:S(2)}, u32[]{:S(2)}) %all-to-all-start.3) | async-done | bytes 262176 | tf_op jit(solution)/shard_map/all_to_all | solution.py:386
  89.6 0.8 backward_kernel.1
  90.4 0.0 copy-start.3
  90.4 5.6 %all-to-all-start.4 = ((f32[64,8,128]{2,1,0:T(8,128)}), f32[64,8,128]{2,1,0:T(8,128)S(1)}, u32[]{:S(2)}, u32[]{:S(2)}) async-start(f32[64,8,128]{2,1,0:T(8,128)} %bitcast.30), calls=%async_computation.4 | async-start | bytes 524288 | tf_op jit(solution)/shard_map/all_to_all | solution.py:386
  96.0 0.0 copy-done.3
  96.0 1.1 %part_kernel.1 = (f32[128,512]{1,0:T(8,128)S(1)}, f32[128,512]{1,0:T(8,128)S(1)}, f32[512,128]{1,0:T(8,128)S(1)}, f32[512,128]{1,0:T(8,128)S(1)}) custom-call(s32[1]{0:T(128)} %bitcast.start_ref, bf16[128,512]{1,0:T(8,128)(2,1)S(1)} %copy-done.2, bf16[128,512]{1,0:T(8,128)(2,1)S(1)} %copy-done, f32[4,128]{1,0:T(4,128)S(1)} %copy-done.5, ...), custom_call_target="tpu_custom_call" | custom-call | tf_op jit(solution)/shard_map/part_kernel/pallas_call | solution.py:368
  97.1 11.1 %all-to-all-done.4 = f32[64,8,128]{2,1,0:T(8,128)S(1)} async-done(((f32[64,8,128]{2,1,0:T(8,128)}), f32[64,8,128]{2,1,0:T(8,128)S(1)}, u32[]{:S(2)}, u32[]{:S(2)}) %all-to-all-start.4) | async-done | bytes 262176 | tf_op jit(solution)/shard_map/all_to_all | solution.py:386
  108.2 0.7 collective-permute-start.1
  108.9 0.0 collective-permute-done.1.edge_ref
  108.9 1.0 final_kernel.1
  (3 shorter events, 0.1 us)
Async XLA Ops:
  0.7 2.3 %collective-permute-start = (f32[512,128]{1,0:T(8,128)S(1)}, f32[512,128]{1,0:T(8,128)S(1)}, u32[]{:S(2)}, u32[]{:S(2)}) collective-permute-start(f32[512,128]{1,0:T(8,128)S(1)} %source_kernel.1), channel_id=1, source_target_pairs={{504,512},{505,513},{506,514},{507,515},{508,516},{509,517},{510,5... | collective-permute-start | bytes 786440 | tf_op jit(solution)/shard_map/ppermute | solution.py:415
  37.0 6.5 %copy-start.5 = (f32[4,128]{1,0:T(4,128)S(1)}, f32[4,128]{1,0:T(4,128)}, u32[]{:S(2)}) copy-start(f32[4,128]{1,0:T(4,128)} %decay_ref.7) | copy-start | bytes 6148
  37.0 6.5 %copy-start.7 = (f32[512]{0:T(512)S(1)}, f32[512]{0:T(512)}, u32[]{:S(2)}) copy-start(f32[512]{0:T(512)} %param.13) | copy-start | bytes 6148
  37.8 5.7 %copy-start = (bf16[128,512]{1,0:T(8,128)(2,1)S(1)}, bf16[128,512]{1,0:T(8,128)(2,1)}, u32[]{:S(2)}) copy-start(bf16[128,512]{1,0:T(8,128)(2,1)} %value_ref.9) | copy-start | bytes 393220
  37.8 5.7 %copy-start.1 = (bf16[128,512]{1,0:T(8,128)(2,1)S(1)}, bf16[128,512]{1,0:T(8,128)(2,1)}, u32[]{:S(2)}) copy-start(bf16[128,512]{1,0:T(8,128)(2,1)} %key_ref.7) | copy-start | bytes 393220
  37.8 5.7 %copy-start.2 = (bf16[128,512]{1,0:T(8,128)(2,1)S(1)}, bf16[128,512]{1,0:T(8,128)(2,1)}, u32[]{:S(2)}) copy-start(bf16[128,512]{1,0:T(8,128)(2,1)} %query_ref.5) | copy-start | bytes 393220
  37.8 5.7 %copy-start.4 = (bf16[128,512]{1,0:T(8,128)(2,1)S(1)}, bf16[128,512]{1,0:T(8,128)(2,1)}, u32[]{:S(2)}) copy-start(bf16[128,512]{1,0:T(8,128)(2,1)} %grad_ref.1) | copy-start | bytes 393220
  37.8 17.9 %all-to-all-start.1 = ((f32[64,8,128]{2,1,0:T(8,128)}), f32[64,8,128]{2,1,0:T(8,128)S(1)}, u32[]{:S(2)}, u32[]{:S(2)}) async-start(f32[64,8,128]{2,1,0:T(8,128)} %bitcast.31), calls=%async_computation.1 | async-start | bytes 524288 | tf_op jit(solution)/shard_map/all_to_all | solution.py:386
  43.5 0.7 copy-start.6
  70.4 19.1 %all-to-all-start.3 = ((f32[64,8,128]{2,1,0:T(8,128)}), f32[64,8,128]{2,1,0:T(8,128)S(1)}, u32[]{:S(2)}, u32[]{:S(2)}) async-start(f32[64,8,128]{2,1,0:T(8,128)} %bitcast.18), calls=%async_computation.3 | async-start | bytes 524288 | tf_op jit(solution)/shard_map/all_to_all | solution.py:386
  90.4 5.6 %copy-start.3 = (f32[512,128]{1,0:T(8,128)S(1)}, f32[512,128]{1,0:T(8,128)}, u32[]{:S(2)}) copy-start(f32[512,128]{1,0:T(8,128)} %get-tuple-element.43.grad_state_ref) | copy-start | bytes 786436
  90.4 17.8 %all-to-all-start.4 = ((f32[64,8,128]{2,1,0:T(8,128)}), f32[64,8,128]{2,1,0:T(8,128)S(1)}, u32[]{:S(2)}, u32[]{:S(2)}) async-start(f32[64,8,128]{2,1,0:T(8,128)} %bitcast.30), calls=%async_computation.4 | async-start | bytes 524288 | tf_op jit(solution)/shard_map/all_to_all | solution.py:386
  108.2 0.7 collective-permute-start.1

commit v6 on v4

--- a/solution.py
+++ b/solution.py
@@ -14,7 +14,8 @@
 F32 = jnp.float32
 BF16 = jnp.bfloat16
 HIGH = lax.Precision.HIGHEST
-GROUPS = [[half * HALF + b for b in range(HALF)] for half in range(2)]
+TURN = 16
+GROUPS = [[half * HALF + (p + TURN) % HALF for p in range(HALF)] for half in range(2)]
 
 
 def dot(a, b, dims, precision=None):
@@ -63,6 +64,10 @@
     def factor(self, h):
         gone = jnp.where(self.doc_last < self.start, jnp.exp(self.last(h)), 0.0)
         return jnp.broadcast_to(gone, (1, DH))
+
+
+def slot(b):
+    return (b - TURN) % HALF
 
 
 def split(x):
@@ -157,8 +162,8 @@
 def forward_kernel(packed_ref, incoming_ref, factor_ref):
     carry = jnp.zeros((SUB, DH), F32)
     for b in range(HALF):
-        at = b * (SUB + 1)
-        rows = pl.ds(b * SUB, SUB)
+        at = slot(b) * (SUB + 1)
+        rows = pl.ds(slot(b) * SUB, SUB)
         factor = jnp.broadcast_to(packed_ref[at + SUB : at + SUB + 1, :], (SUB, DH))
         incoming_ref[rows, :] = carry
         factor_ref[rows, :] = factor
@@ -168,7 +173,7 @@
 def backward_kernel(grad_ref, factor_ref, outgoing_ref):
     carry = jnp.zeros((SUB, DH), F32)
     for b in reversed(range(HALF)):
-        rows = pl.ds(b * SUB, SUB)
+        rows = pl.ds(slot(b) * SUB, SUB)
         outgoing_ref[rows, :] = carry
         carry = factor_ref[rows, :] * carry + grad_ref[rows, :]
 

time: 111 us -> 110 us (level)
  starting transfers between devices: 19.3 us -> 21.3 us
  waiting for transfers between devices: 31.4 us -> 29.4 us
    all_to_all x3, waiting for transfers between devices: 31.4 us -> 29.4 us  [exchange(): lax.all_to_all(rows.reshape(shape), 'ctx', 0, 0, axis_index_groups=GROUPS...]
    all_to_all x3, starting transfers between devices: 18 us -> 19.9 us  [exchange(): lax.all_to_all(rows.reshape(shape), 'ctx', 0, 0, axis_index_groups=GROUPS...]
where the time goes in v6:
time: 110 us; the launch traced here: 109 us
  blocking collectives  46.9 us (43%)
  waiting for transfers between devices  29.4 us (27%)
  starting transfers between devices  21.3 us (19%)
  Pallas kernels  10.5 us (10%)
    all_to_all x1, blocking collectives, exchange(): lax.all_to_all(rows.reshape(shape), 'ctx', 0, 0, axis_index_groups=GROUPS...  33.7 us
    all_to_all x3, waiting for transfers between devices, exchange(): lax.all_to_all(rows.reshape(shape), 'ctx', 0, 0, axis_index_groups=GROUPS...  29.4 us
    all_to_all x3, starting transfers between devices, exchange(): lax.all_to_all(rows.reshape(shape), 'ctx', 0, 0, axis_index_groups=GROUPS...  19.9 us
    all_to_all x1, blocking collectives, on_device(): lax.all_to_all(sums.reshape(peers, SUB, DH), 'head', 0, 0, tiled=True)  13.2 us
    pallas_call x11, Pallas kernels, call(): pl.pallas_call(kernel, out_shape=tuple((pltpu.VMEM(shape, kind) if keep e...  10.4 us
  transfers between devices with their start and end apart: 5, of which 3 were waited for; matrix products, arithmetic and copies ran while one was open for 0% of the time, Pallas kernels for 6%

profile of v6, /device:TPU:1, one launch (start us, length us, event | category | flops | bytes accessed | tf_op | source)
XLA Modules:
  0.0 109.5 jit_solution(17032047786948225141)
XLA Ops:
  0.7 0.7 collective-permute-start
  1.4 1.6 %local_kernel.1 = (f32[512,128]{1,0:T(8,128)S(1)}, f32[4,128]{1,0:T(4,128)S(1)}) custom-call(s32[1]{0:T(128)} %bitcast.start_ref, bf16[128,512]{1,0:T(8,128)(2,1)} %key_ref.7, bf16[128,512]{1,0:T(8,128)(2,1)} %value_ref.9, f32[4,128]{1,0:T(4,128)} %decay_ref.7, s32[1,128]{1,0:T(1,128)} %bitcast.23), custom_call_target="tpu_custom_call" | custom-call | tf_op jit(solution)/shard_map/local_kernel/pallas_call | solution.py:332
  3.0 0.0 collective-permute-done.edge_ref
  3.0 33.7 %all_to_all.25 = f32[64,9,1,128]{3,2,1,0:T(1,128)S(1)} all-to-all(f32[64,9,1,128]{3,2,1,0:T(1,128)S(1)} %bitcast.15), channel_id=1, replica_groups={{128,136,144,152,160,168,176,184,192,200,208,216,224,232,240,248,256,26..., dimensions={0} | all-to-all | bytes 589824 | tf_op jit(solution)/shard_map/all_to_all | solution.py:346
  36.7 0.0 copy-start.4
  36.7 0.0 copy-start.6
  36.7 0.8 forward_kernel.1
  37.6 0.0 copy-start
  37.6 0.0 copy-start.1
  37.6 0.0 copy-start.2
  37.6 0.0 copy-start.3
  37.6 6.3 %all-to-all-start.1 = ((f32[64,8,128]{2,1,0:T(8,128)}), f32[64,8,128]{2,1,0:T(8,128)S(1)}, u32[]{:S(2)}, u32[]{:S(2)}) async-start(f32[64,8,128]{2,1,0:T(8,128)} %bitcast.5), calls=%async_computation.1 | async-start | bytes 524288 | tf_op jit(solution)/shard_map/all_to_all | solution.py:346
  43.9 0.0 copy-start.5
  43.9 0.0 copy-done.4
  43.9 0.0 copy-done.6
  43.9 0.0 copy-done
  43.9 0.0 copy-done.1
  43.9 0.0 copy-done.2
  43.9 0.0 copy-done.3
  43.9 0.6 copy-done.5
  44.5 1.0 inner_kernel.1
  45.5 9.9 %all-to-all-done.1 = f32[64,8,128]{2,1,0:T(8,128)S(1)} async-done(((f32[64,8,128]{2,1,0:T(8,128)}), f32[64,8,128]{2,1,0:T(8,128)S(1)}, u32[]{:S(2)}, u32[]{:S(2)}) %all-to-all-start.1) | async-done | bytes 262176 | tf_op jit(solution)/shard_map/all_to_all | solution.py:346
  55.4 0.5 output_kernel.1
  55.9 13.2 %all_to_all.26 = f32[8,8,128]{2,1,0:T(8,128)S(1)} all-to-all(f32[8,8,128]{2,1,0:T(8,128)S(1)} %bitcast.21), channel_id=1, replica_groups=mesh['ctx'=128,'head'=8] {'head'}, dimensions={0} | all-to-all | bytes 65536 | tf_op jit(solution)/shard_map/all_to_all | solution.py:414
  69.2 1.0 grad_kernel.1
  70.2 7.5 %all-to-all-start.3 = ((f32[64,8,128]{2,1,0:T(8,128)}), f32[64,8,128]{2,1,0:T(8,128)S(1)}, u32[]{:S(2)}, u32[]{:S(2)}) async-start(f32[64,8,128]{2,1,0:T(8,128)} %bitcast.9), calls=%async_computation.3 | async-start | bytes 524288 | tf_op jit(solution)/shard_map/all_to_all | solution.py:346
  77.7 1.5 %intra_kernel.1 = (bf16[128,512]{1,0:T(8,128)(2,1)}, bf16[128,512]{1,0:T(8,128)(2,1)}) custom-call(s32[1]{0:T(128)} %bitcast.start_ref, bf16[128,512]{1,0:T(8,128)(2,1)S(1)} %copy-done.1, bf16[128,512]{1,0:T(8,128)(2,1)S(1)} %copy-done, f32[1,512]{1,0:T(1,128)S(1)} %bitcast.28, f32[4,128]{1,0:T(4,128)S(1)} %copy-done.4, s32[1,128]{1,0:T(1,128)S(1)} %bitcast.25, ...), custom_call_target="tpu_custom_call" | custom-call | tf_op jit(solution)/shard_map/intra_kernel/pallas_call | solution.py:332
  79.2 10.0 %all-to-all-done.3 = f32[64,8,128]{2,1,0:T(8,128)S(1)} async-done(((f32[64,8,128]{2,1,0:T(8,128)}), f32[64,8,128]{2,1,0:T(8,128)S(1)}, u32[]{:S(2)}, u32[]{:S(2)}) %all-to-all-start.3) | async-done | bytes 262176 | tf_op jit(solution)/shard_map/all_to_all | solution.py:346
  89.2 0.8 backward_kernel.1
  90.0 6.1 %all-to-all-start.4 = ((f32[64,8,128]{2,1,0:T(8,128)}), f32[64,8,128]{2,1,0:T(8,128)S(1)}, u32[]{:S(2)}, u32[]{:S(2)}) async-start(f32[64,8,128]{2,1,0:T(8,128)} %bitcast.11), calls=%async_computation.4 | async-start | bytes 524288 | tf_op jit(solution)/shard_map/all_to_all | solution.py:346
  96.2 2.1 %part_kernel.1 = (f32[128,512]{1,0:T(8,128)S(1)}, f32[128,512]{1,0:T(8,128)S(1)}, f32[512,128]{1,0:T(8,128)S(1)}, f32[512,128]{1,0:T(8,128)S(1)}) custom-call(s32[1]{0:T(128)} %bitcast.start_ref, bf16[128,512]{1,0:T(8,128)(2,1)S(1)} %copy-done.2, bf16[128,512]{1,0:T(8,128)(2,1)S(1)} %copy-done, f32[4,128]{1,0:T(4,128)S(1)} %copy-done.4, ...), custom_call_target="tpu_custom_call" | custom-call | tf_op jit(solution)/shard_map/part_kernel/pallas_call | solution.py:332
  98.3 9.5 %all-to-all-done.4 = f32[64,8,128]{2,1,0:T(8,128)S(1)} async-done(((f32[64,8,128]{2,1,0:T(8,128)}), f32[64,8,128]{2,1,0:T(8,128)S(1)}, u32[]{:S(2)}, u32[]{:S(2)}) %all-to-all-start.4) | async-done | bytes 262176 | tf_op jit(solution)/shard_map/all_to_all | solution.py:346
  107.8 0.7 collective-permute-start.1
  108.5 0.0 collective-permute-done.1.edge_ref
  108.5 1.0 final_kernel.1
  (3 shorter events, 0.1 us)
Async XLA Ops:
  0.7 2.3 %collective-permute-start = (f32[512,128]{1,0:T(8,128)S(1)}, f32[512,128]{1,0:T(8,128)S(1)}, u32[]{:S(2)}, u32[]{:S(2)}) collective-permute-start(f32[512,128]{1,0:T(8,128)S(1)} %source_kernel.1), channel_id=1, source_target_pairs={{504,512},{505,513},{506,514},{507,515},{508,516},{509,517},{510,5... | collective-permute-start | bytes 786440 | tf_op jit(solution)/shard_map/ppermute | solution.py:375
  36.7 7.1 %copy-start.4 = (f32[4,128]{1,0:T(4,128)S(1)}, f32[4,128]{1,0:T(4,128)}, u32[]{:S(2)}) copy-start(f32[4,128]{1,0:T(4,128)} %decay_ref.7) | copy-start | bytes 6148
  36.7 7.2 %copy-start.6 = (f32[512]{0:T(512)S(1)}, f32[512]{0:T(512)}, u32[]{:S(2)}) copy-start(f32[512]{0:T(512)} %param.13) | copy-start | bytes 6148
  37.6 6.3 %copy-start = (bf16[128,512]{1,0:T(8,128)(2,1)S(1)}, bf16[128,512]{1,0:T(8,128)(2,1)}, u32[]{:S(2)}) copy-start(bf16[128,512]{1,0:T(8,128)(2,1)} %value_ref.9) | copy-start | bytes 393220
  37.6 6.3 %copy-start.1 = (bf16[128,512]{1,0:T(8,128)(2,1)S(1)}, bf16[128,512]{1,0:T(8,128)(2,1)}, u32[]{:S(2)}) copy-start(bf16[128,512]{1,0:T(8,128)(2,1)} %key_ref.7) | copy-start | bytes 393220
  37.6 6.3 %copy-start.2 = (bf16[128,512]{1,0:T(8,128)(2,1)S(1)}, bf16[128,512]{1,0:T(8,128)(2,1)}, u32[]{:S(2)}) copy-start(bf16[128,512]{1,0:T(8,128)(2,1)} %query_ref.5) | copy-start | bytes 393220
  37.6 6.4 %copy-start.3 = (bf16[128,512]{1,0:T(8,128)(2,1)S(1)}, bf16[128,512]{1,0:T(8,128)(2,1)}, u32[]{:S(2)}) copy-start(bf16[128,512]{1,0:T(8,128)(2,1)} %grad_ref.1) | copy-start | bytes 393220
  37.6 17.8 %all-to-all-start.1 = ((f32[64,8,128]{2,1,0:T(8,128)}), f32[64,8,128]{2,1,0:T(8,128)S(1)}, u32[]{:S(2)}, u32[]{:S(2)}) async-start(f32[64,8,128]{2,1,0:T(8,128)} %bitcast.5), calls=%async_computation.1 | async-start | bytes 524288 | tf_op jit(solution)/shard_map/all_to_all | solution.py:346
  43.9 0.7 copy-start.5
  70.2 19.0 %all-to-all-start.3 = ((f32[64,8,128]{2,1,0:T(8,128)}), f32[64,8,128]{2,1,0:T(8,128)S(1)}, u32[]{:S(2)}, u32[]{:S(2)}) async-start(f32[64,8,128]{2,1,0:T(8,128)} %bitcast.9), calls=%async_computation.3 | async-start | bytes 524288 | tf_op jit(solution)/shard_map/all_to_all | solution.py:346
  90.0 17.7 %all-to-all-start.4 = ((f32[64,8,128]{2,1,0:T(8,128)}), f32[64,8,128]{2,1,0:T(8,128)S(1)}, u32[]{:S(2)}, u32[]{:S(2)}) async-start(f32[64,8,128]{2,1,0:T(8,128)} %bitcast.11), calls=%async_computation.4 | async-start | bytes 524288 | tf_op jit(solution)/shard_map/all_to_all | solution.py:346
  107.8 0.7 collective-permute-start.1

commit v7 on v6

--- a/solution.py
+++ b/solution.py
@@ -113,15 +113,7 @@
             local_ref[h * DH : (h + 1) * DH, :] = dot(weighted, head(value_ref, h), ((0,), (0,)))
 
 
-def local_kernel(start_ref, key_ref, value_ref, decay_ref, doc_ref, local_ref, factor_ref):
-    t = Tables(decay_ref, doc_ref, start_ref)
-    for h in range(t.heads):
-        weighted = (head(key_ref, h).astype(F32) * t.outward(h)).astype(BF16)
-        local_ref[h * DH : (h + 1) * DH, :] = dot(weighted, head(value_ref, h), ((0,), (0,)))
-        factor_ref[h : h + 1, :] = t.factor(h)
-
-
-def inner_kernel(
+def local_kernel(
     start_ref,
     query_ref,
     key_ref,
@@ -130,6 +122,8 @@
     gain_ref,
     decay_ref,
     doc_ref,
+    local_ref,
+    factor_ref,
     attend_ref,
     inner_ref,
     inward_ref,
@@ -138,13 +132,15 @@
 ):
     t = Tables(decay_ref, doc_ref, start_ref)
     for h in range(t.heads):
-        decay = t.decay(h)
+        weighted = (head(key_ref, h).astype(F32) * t.outward(h)).astype(BF16)
+        local_ref[h * DH : (h + 1) * DH, :] = dot(weighted, head(value_ref, h), ((0,), (0,)))
+        factor_ref[h : h + 1, :] = t.factor(h)
         inward = t.inward(h)
         inward_ref[h * DH : (h + 1) * DH, :] = inward
         gated_ref[:, h * DH : (h + 1) * DH] = (head(query_ref, h).astype(F32) * inward).astype(BF16)
         scaled_ref[:, h * DH : (h + 1) * DH] = head(grad_ref, h).astype(F32) * head(gain_ref, h)
         scores = dot(head(query_ref, h), head(key_ref, h), ((1,), (1,)))
-        attend = (scores * decay).astype(BF16)
+        attend = (scores * t.decay(h)).astype(BF16)
         attend_ref[h * DH : (h + 1) * DH, :] = attend
         inner_ref[:, h * DH : (h + 1) * DH] = dot(attend, head(value_ref, h), ((1,), (0,)))
 
@@ -373,19 +369,17 @@
         name="source_kernel",
     )(start, key_rows, value_rows, *decays)
     edge = lax.ppermute(source, "ctx", [(HALF - 1, HALF)])
-    local, factor = call(
+    local, factor, attend, inner, inward, gated, scaled = call(
         local_kernel,
-        (states, ((heads, DH), F32, True)),
-        start,
-        key_rows,
-        value_rows,
-        *decays,
-        scalars=1,
-        pinned=False,
-    )
-    attend, inner, inward, gated, scaled = call(
-        inner_kernel,
-        (((heads * DH, DH), BF16, True), wide, states, narrow, wide),
+        (
+            states,
+            ((heads, DH), F32, True),
+            ((heads * DH, DH), BF16, True),
+            wide,
+            states,
+            narrow,
+            wide,
+        ),
         start,
         queries,
         key_rows,
@@ -394,6 +388,7 @@
         gains,
         *decays,
         scalars=1,
+        pinned=False,
     )
     (packed,) = call(pack_kernel, (((HALF * (SUB + 1), DH), F32, True),), local, factor, edge)
     packed = exchange(packed, SUB + 1)

time: 110 us -> 111 us (level)
  the two profiles are of different devices: /device:TPU:1 before, /device:TPU:497 now
where the time goes in v7:
time: 111 us
  blocking collectives  47.8 us (43%)
  waiting for transfers between devices  27.9 us (25%)
  starting transfers between devices  22.3 us (20%)
  Pallas kernels  11.3 us (10%)
    all_to_all x2, blocking collectives, exchange(): lax.all_to_all(rows.reshape(shape), 'ctx', 0, 0, axis_index_groups=GROUPS...  34.6 us
    all_to_all x2, starting transfers between devices, exchange(): lax.all_to_all(rows.reshape(shape), 'ctx', 0, 0, axis_index_groups=GROUPS...  17.5 us
    all_to_all x2, waiting for transfers between devices, exchange(): lax.all_to_all(rows.reshape(shape), 'ctx', 0, 0, axis_index_groups=GROUPS...  15.1 us
    all_to_all x1, blocking collectives, on_device(): lax.all_to_all(sums.reshape(peers, SUB, DH), 'head', 0, 0, tiled=True)  13.2 us
    ppermute x1, waiting for transfers between devices, on_device(): after = lax.ppermute(before, 'ctx', [(HALF, HALF - 1)])  11.9 us
    pallas_call x10, Pallas kernels, call(): pl.pallas_call(kernel, out_shape=tuple((pltpu.VMEM(shape, kind) if keep e...  9.59 us
    ppermute x1, starting transfers between devices, on_device(): edge = lax.ppermute(source, 'ctx', [(HALF - 1, HALF)])  3.48 us
  transfers between devices with their start and end apart: 4, of which 4 were waited for; matrix products, arithmetic and copies ran while one was open for 0% of the time, Pallas kernels for 5%

profile of v7, /device:TPU:497, one launch (start us, length us, event | category | flops | bytes accessed | tf_op | source)
XLA Modules:
  0.0 110.6 jit_solution(2546996119417501513)
XLA Ops:
  0.6 1.7 %source_kernel.1 = f32[512,128]{1,0:T(8,128)S(1)} custom-call(s32[1]{0:T(128)} %bitcast.start_ref, bf16[128,512]{1,0:T(8,128)(2,1)} %key_ref.5, bf16[128,512]{1,0:T(8,128)(2,1)} %value_ref.7, f32[4,128]{1,0:T(4,128)} %decay_ref.5, s32[1,128]{1,0:T(1,128)} %bitcast.25), custom_call_target="tpu_custom_call" | custom-call | tf_op jit(solution)/shard_map/source_kernel/pallas_call | solution.py:360
  2.3 3.5 %collective-permute-start = (f32[512,128]{1,0:T(8,128)S(1)}, f32[512,128]{1,0:T(8,128)S(1)}, u32[]{:S(2)}, u32[]{:S(2)}) collective-permute-start(f32[512,128]{1,0:T(8,128)S(1)} %source_kernel.1), channel_id=1, source_target_pairs={{504,512},{505,513},{506,514},{507,515},{508,516},{509,517},{510,5... | collective-permute-start | bytes 786440 | tf_op jit(solution)/shard_map/ppermute | solution.py:371
  5.8 2.4 %local_kernel.1 = (f32[512,128]{1,0:T(8,128)S(1)}, f32[4,128]{1,0:T(4,128)S(1)}, bf16[512,128]{1,0:T(8,128)(2,1)S(1)}, f32[128,512]{1,0:T(8,128)S(1)}, f32[512,1...) custom-call(s32[1]{0:T(128)} %bitcast.start_ref, bf16[128,512]{1,0:T(8,128)(2,1)} %query_ref.5, ...), custom_call_target="tpu_custom_call" | custom-call | tf_op jit(solution)/shard_map/local_kernel/pallas_call | solution.py:328
  8.2 0.0 copy-start.3
  8.2 0.9 collective-permute-done.edge_ref
  9.1 0.0 copy-done.3
  9.1 17.0 %all_to_all.25 = f32[64,9,1,128]{3,2,1,0:T(1,128)S(1)} all-to-all(f32[64,9,1,128]{3,2,1,0:T(1,128)S(1)} %bitcast.15), channel_id=1, replica_groups={{128,136,144,152,160,168,176,184,192,200,208,216,224,232,240,248,256,26..., dimensions={0} | all-to-all | bytes 589824 | tf_op jit(solution)/shard_map/all_to_all | solution.py:342
  26.1 0.1 forward_kernel.1
  26.3 0.0 copy-start.2
  26.3 17.6 %all_to_all.26 = f32[64,8,128]{2,1,0:T(8,128)S(1)} all-to-all(f32[64,8,128]{2,1,0:T(8,128)S(1)} %bitcast.21), channel_id=1, replica_groups={{128,136,144,152,160,168,176,184,192,200,208,216,224,232,240,248,256,26..., dimensions={0} | all-to-all | bytes 524288 | tf_op jit(solution)/shard_map/all_to_all | solution.py:342
  43.9 0.0 copy-done.2
  43.9 0.0 copy-start.4
  43.9 0.5 output_kernel.1
  44.4 13.2 %all_to_all.27 = f32[8,8,128]{2,1,0:T(8,128)S(1)} all-to-all(f32[8,8,128]{2,1,0:T(8,128)S(1)} %bitcast.22), channel_id=1, replica_groups=mesh['ctx'=128,'head'=8] {'head'}, dimensions={0} | all-to-all | bytes 65536 | tf_op jit(solution)/shard_map/all_to_all | solution.py:409
  57.6 0.0 copy-done.4
  57.6 1.0 grad_kernel.1
  58.6 0.0 copy-start
  58.6 0.0 copy-start.1
  58.6 0.0 copy-start.6
  58.6 9.5 %all-to-all-start.3 = ((f32[64,8,128]{2,1,0:T(8,128)}), f32[64,8,128]{2,1,0:T(8,128)S(1)}, u32[]{:S(2)}, u32[]{:S(2)}) async-start(f32[64,8,128]{2,1,0:T(8,128)} %bitcast.9), calls=%async_computation.3 | async-start | bytes 524288 | tf_op jit(solution)/shard_map/all_to_all | solution.py:342
  68.1 0.0 copy-start.5
  68.1 0.0 copy-start.7
  68.1 0.0 copy-done
  68.2 0.0 copy-done.1
  68.2 0.0 copy-done.6
  68.2 0.6 copy-done.5
  68.8 0.0 copy-done.7
  68.8 1.5 %intra_kernel.1 = (bf16[128,512]{1,0:T(8,128)(2,1)}, bf16[128,512]{1,0:T(8,128)(2,1)}) custom-call(s32[1]{0:T(128)} %bitcast.start_ref, bf16[128,512]{1,0:T(8,128)(2,1)S(1)} %copy-done.1, bf16[128,512]{1,0:T(8,128)(2,1)S(1)} %copy-done, f32[1,512]{1,0:T(1,128)S(1)} %bitcast.24, f32[4,128]{1,0:T(4,128)S(1)} %copy-done.5, s32[1,128]{1,0:T(1,128)S(1)} %bitcast.27, ...), custom_call_target="tpu_custom_call" | custom-call | tf_op jit(solution)/shard_map/intra_kernel/pallas_call | solution.py:328
  70.4 7.5 %all-to-all-done.3 = f32[64,8,128]{2,1,0:T(8,128)S(1)} async-done(((f32[64,8,128]{2,1,0:T(8,128)}), f32[64,8,128]{2,1,0:T(8,128)S(1)}, u32[]{:S(2)}, u32[]{:S(2)}) %all-to-all-start.3) | async-done | bytes 262176 | tf_op jit(solution)/shard_map/all_to_all | solution.py:342
  77.8 0.8 backward_kernel.1
  78.7 8.0 %all-to-all-start.4 = ((f32[64,8,128]{2,1,0:T(8,128)}), f32[64,8,128]{2,1,0:T(8,128)S(1)}, u32[]{:S(2)}, u32[]{:S(2)}) async-start(f32[64,8,128]{2,1,0:T(8,128)} %bitcast.11), calls=%async_computation.4 | async-start | bytes 524288 | tf_op jit(solution)/shard_map/all_to_all | solution.py:342
  86.7 2.1 %part_kernel.1 = (f32[128,512]{1,0:T(8,128)S(1)}, f32[128,512]{1,0:T(8,128)S(1)}, f32[512,128]{1,0:T(8,128)S(1)}, f32[512,128]{1,0:T(8,128)S(1)}) custom-call(s32[1]{0:T(128)} %bitcast.start_ref, bf16[128,512]{1,0:T(8,128)(2,1)S(1)} %copy-done.2, bf16[128,512]{1,0:T(8,128)(2,1)S(1)} %copy-done, f32[4,128]{1,0:T(4,128)S(1)} %copy-done.5, ...), custom_call_target="tpu_custom_call" | custom-call | tf_op jit(solution)/shard_map/part_kernel/pallas_call | solution.py:328
  88.7 7.6 %all-to-all-done.4 = f32[64,8,128]{2,1,0:T(8,128)S(1)} async-done(((f32[64,8,128]{2,1,0:T(8,128)}), f32[64,8,128]{2,1,0:T(8,128)S(1)}, u32[]{:S(2)}, u32[]{:S(2)}) %all-to-all-start.4) | async-done | bytes 262176 | tf_op jit(solution)/shard_map/all_to_all | solution.py:342
  96.4 1.3 %collective-permute-start.1 = (f32[512,128]{1,0:T(8,128)S(1)}, f32[512,128]{1,0:T(8,128)S(1)}, u32[]{:S(2)}, u32[]{:S(2)}) collective-permute-start(f32[512,128]{1,0:T(8,128)S(1)} %edge_kernel.1), channel_id=1, source_target_pairs={{512,504},{513,505},{514,506},{515,507},{516,508},{517,509},{518,5... | collective-permute-start | bytes 786440 | tf_op jit(solution)/shard_map/ppermute | solution.py:449
  97.7 11.9 %collective-permute-done.1.edge_ref = f32[512,128]{1,0:T(8,128)S(1)} collective-permute-done((f32[512,128]{1,0:T(8,128)S(1)}, f32[512,128]{1,0:T(8,128)S(1)}, u32[]{:S(2)}, u32[]{:S(2)}) %collective-permute-start.1) | collective-permute-done | bytes 262176 | tf_op jit(solution)/shard_map/ppermute | solution.py:449
  109.6 1.0 final_kernel.1
  (2 shorter events, 0.1 us)
Async XLA Ops:
  2.3 6.8 %collective-permute-start = (f32[512,128]{1,0:T(8,128)S(1)}, f32[512,128]{1,0:T(8,128)S(1)}, u32[]{:S(2)}, u32[]{:S(2)}) collective-permute-start(f32[512,128]{1,0:T(8,128)S(1)} %source_kernel.1), channel_id=1, source_target_pairs={{504,512},{505,513},{506,514},{507,515},{508,516},{509,517},{510,5... | collective-permute-start | bytes 786440 | tf_op jit(solution)/shard_map/ppermute | solution.py:371
  8.2 0.9 copy-start.3
  26.3 17.6 %copy-start.2 = (bf16[128,512]{1,0:T(8,128)(2,1)S(1)}, bf16[128,512]{1,0:T(8,128)(2,1)}, u32[]{:S(2)}) copy-start(bf16[128,512]{1,0:T(8,128)(2,1)} %query_ref.5) | copy-start | bytes 393220
  43.9 13.7 %copy-start.4 = (bf16[128,512]{1,0:T(8,128)(2,1)S(1)}, bf16[128,512]{1,0:T(8,128)(2,1)}, u32[]{:S(2)}) copy-start(bf16[128,512]{1,0:T(8,128)(2,1)} %copy-done.3) | copy-start | bytes 393220
  58.6 9.6 %copy-start = (bf16[128,512]{1,0:T(8,128)(2,1)S(1)}, bf16[128,512]{1,0:T(8,128)(2,1)}, u32[]{:S(2)}) copy-start(bf16[128,512]{1,0:T(8,128)(2,1)} %value_ref.7) | copy-start | bytes 393220
  58.6 9.6 %copy-start.1 = (bf16[128,512]{1,0:T(8,128)(2,1)S(1)}, bf16[128,512]{1,0:T(8,128)(2,1)}, u32[]{:S(2)}) copy-start(bf16[128,512]{1,0:T(8,128)(2,1)} %key_ref.5) | copy-start | bytes 393220
  58.6 9.6 %copy-start.6 = (f32[512]{0:T(512)S(1)}, f32[512]{0:T(512)}, u32[]{:S(2)}) copy-start(f32[512]{0:T(512)} %param.13) | copy-start | bytes 6148
  58.6 19.2 %all-to-all-start.3 = ((f32[64,8,128]{2,1,0:T(8,128)}), f32[64,8,128]{2,1,0:T(8,128)S(1)}, u32[]{:S(2)}, u32[]{:S(2)}) async-start(f32[64,8,128]{2,1,0:T(8,128)} %bitcast.9), calls=%async_computation.3 | async-start | bytes 524288 | tf_op jit(solution)/shard_map/all_to_all | solution.py:342
  68.1 0.7 copy-start.5
  68.1 0.7 copy-start.7
  78.7 17.7 %all-to-all-start.4 = ((f32[64,8,128]{2,1,0:T(8,128)}), f32[64,8,128]{2,1,0:T(8,128)S(1)}, u32[]{:S(2)}, u32[]{:S(2)}) async-start(f32[64,8,128]{2,1,0:T(8,128)} %bitcast.11), calls=%async_computation.4 | async-start | bytes 524288 | tf_op jit(solution)/shard_map/all_to_all | solution.py:342
  96.4 13.2 %collective-permute-start.1 = (f32[512,128]{1,0:T(8,128)S(1)}, f32[512,128]{1,0:T(8,128)S(1)}, u32[]{:S(2)}, u32[]{:S(2)}) collective-permute-start(f32[512,128]{1,0:T(8,128)S(1)} %edge_kernel.1), channel_id=1, source_target_pairs={{512,504},{513,505},{514,506},{515,507},{516,508},{517,509},{518,5... | collective-permute-start | bytes 786440 | tf_op jit(solution)/shard_map/ppermute | solution.py:449

commit v8 on v7

--- a/solution.py
+++ b/solution.py
@@ -127,7 +127,6 @@
     attend_ref,
     inner_ref,
     inward_ref,
-    gated_ref,
     scaled_ref,
 ):
     t = Tables(decay_ref, doc_ref, start_ref)
@@ -135,9 +134,7 @@
         weighted = (head(key_ref, h).astype(F32) * t.outward(h)).astype(BF16)
         local_ref[h * DH : (h + 1) * DH, :] = dot(weighted, head(value_ref, h), ((0,), (0,)))
         factor_ref[h : h + 1, :] = t.factor(h)
-        inward = t.inward(h)
-        inward_ref[h * DH : (h + 1) * DH, :] = inward
-        gated_ref[:, h * DH : (h + 1) * DH] = (head(query_ref, h).astype(F32) * inward).astype(BF16)
+        inward_ref[h * DH : (h + 1) * DH, :] = t.inward(h)
         scaled_ref[:, h * DH : (h + 1) * DH] = head(grad_ref, h).astype(F32) * head(gain_ref, h)
         scores = dot(head(query_ref, h), head(key_ref, h), ((1,), (1,)))
         attend = (scores * t.decay(h)).astype(BF16)
@@ -183,6 +180,7 @@
     edge_ref,
     output_ref,
     state_ref,
+    gated_ref,
     sums_ref,
 ):
     square = jnp.zeros((DH, DH), F32)
@@ -192,7 +190,9 @@
         state_ref[h * DH : (h + 1) * DH, :] = jnp.concatenate([high, low], axis=1)
         stacked = jnp.concatenate([high, low], axis=0)
         carried = dot(twice(head(query_ref, h)), stacked, ((1,), (0,)))
-        output = head(inner_ref, h) + state(inward_ref, h) * carried
+        inward = state(inward_ref, h)
+        gated_ref[:, h * DH : (h + 1) * DH] = (head(query_ref, h).astype(F32) * inward).astype(BF16)
+        output = head(inner_ref, h) + inward * carried
         output_ref[:, h * DH : (h + 1) * DH] = output
         square = square + output * output
         cross = cross + head(scaled_ref, h) * output
@@ -369,7 +369,7 @@
         name="source_kernel",
     )(start, key_rows, value_rows, *decays)
     edge = lax.ppermute(source, "ctx", [(HALF - 1, HALF)])
-    local, factor, attend, inner, inward, gated, scaled = call(
+    local, factor, attend, inner, inward, scaled = call(
         local_kernel,
         (
             states,
@@ -377,7 +377,6 @@
             ((heads * DH, DH), BF16, True),
             wide,
             states,
-            narrow,
             wide,
         ),
         start,
@@ -396,9 +395,9 @@
     incoming = exchange(incoming, SUB)
 
     peers = lax.axis_size("head")
-    output, inbound, sums = call(
+    output, inbound, gated, sums = call(
         output_kernel,
-        (wide, ((heads * DH, 2 * DH), BF16, True), ((peers * SUB, DH), F32, True)),
+        (wide, ((heads * DH, 2 * DH), BF16, True), narrow, ((peers * SUB, DH), F32, True)),
         queries,
         scaled,
         inward,
@@ -427,9 +426,6 @@
         sums,
         scalars=1,
     )
-    arrived, normed, query_grad = lax.optimization_barrier((arrived, normed, query_grad))
-    (outgoing,) = call(backward_kernel, (pieces,), arrived, factors)
-    outgoing = exchange(outgoing, SUB)
     key_part, value_part, outward, own = call(
         part_kernel,
         (wide, wide, states, states),
@@ -442,9 +438,11 @@
         grad_state,
         scalars=1,
     )
-    outgoing, key_part, value_part, outward, own = lax.optimization_barrier(
-        (outgoing, key_part, value_part, outward, own)
-    )
+    arrived, normed, query_grad, key_part, value_part, outward, own = lax.optimization_barrier(
+        (arrived, normed, query_grad, key_part, value_part, outward, own)
+    )
+    (outgoing,) = call(backward_kernel, (pieces,), arrived, factors)
+    outgoing = exchange(outgoing, SUB)
     (before,) = call(edge_kernel, (states,), outgoing, own, factor)
     after = lax.ppermute(before, "ctx", [(HALF, HALF - 1)])
     key_grad, value_grad = call(

time: 111 us -> 110 us (level)
  the two profiles are of different devices: /device:TPU:497 before, /device:TPU:1 now
where the time goes in v8:
time: 110 us; the launch traced here: 108 us
  blocking collectives  81.2 us (74%)
  starting transfers between devices  9.11 us (8%)
  Pallas kernels  8.92 us (8%)
  waiting for transfers between devices  7.24 us (7%)
    all_to_all x3, blocking collectives, exchange(): lax.all_to_all(rows.reshape(shape), 'ctx', 0, 0, axis_index_groups=GROUPS...  68 us
    all_to_all x1, blocking collectives, on_device(): lax.all_to_all(sums.reshape(peers, SUB, DH), 'head', 0, 0, tiled=True)  13.2 us
    pallas_call x10, Pallas kernels, call(): pl.pallas_call(kernel, out_shape=tuple((pltpu.VMEM(shape, kind) if keep e...  8.87 us
    all_to_all x1, starting transfers between devices, exchange(): lax.all_to_all(rows.reshape(shape), 'ctx', 0, 0, axis_index_groups=GROUPS...  7.62 us
    all_to_all x1, waiting for transfers between devices, exchange(): lax.all_to_all(rows.reshape(shape), 'ctx', 0, 0, axis_index_groups=GROUPS...  7.23 us
  transfers between devices with their start and end apart: 3, of which 1 were waited for; matrix products, arithmetic and copies ran while one was open for 0% of the time, Pallas kernels for 6%

profile of v8, /device:TPU:1, one launch (start us, length us, event | category | flops | bytes accessed | tf_op | source)
XLA Modules:
  0.0 108.0 jit_solution(11655462985414356114)
XLA Ops:
  0.7 0.7 collective-permute-start
  1.4 2.4 %local_kernel.1 = (f32[512,128]{1,0:T(8,128)S(1)}, f32[4,128]{1,0:T(4,128)S(1)}, bf16[512,128]{1,0:T(8,128)(2,1)S(1)}, f32[128,512]{1,0:T(8,128)S(1)}, f32[512,128]{1,0:T(8,128)S(1)}, /*index=5*/f32[128,512]{1,0:T(8,128)S(1)}) custom-call(s32[1]{0:T(128)} %bitcast.start_ref, bf16[128,512]{1,0:T(8,128)(2,1)} %query_ref.5, bf16[128,512]{1,0:T(8,128)(2,1)} %key_ref.5, ...), custom_call_target="tpu_custom_call" | custom-call | tf_op jit(solution)/shard_map/local_kernel/pallas_call | solution.py:328
  3.8 0.0 collective-permute-done.edge_ref
  3.8 32.9 %all_to_all.25 = f32[64,9,1,128]{3,2,1,0:T(1,128)S(1)} all-to-all(f32[64,9,1,128]{3,2,1,0:T(1,128)S(1)} %bitcast.15), channel_id=1, replica_groups={{128,136,144,152,160,168,176,184,192,200,208,216,224,232,240,248,256,26..., dimensions={0} | all-to-all | bytes 589824 | tf_op jit(solution)/shard_map/all_to_all | solution.py:342
  36.7 0.1 forward_kernel.1
  36.9 0.0 copy-start.2
  36.9 17.6 %all_to_all.26 = f32[64,8,128]{2,1,0:T(8,128)S(1)} all-to-all(f32[64,8,128]{2,1,0:T(8,128)S(1)} %bitcast.22), channel_id=1, replica_groups={{128,136,144,152,160,168,176,184,192,200,208,216,224,232,240,248,256,26..., dimensions={0} | all-to-all | bytes 524288 | tf_op jit(solution)/shard_map/all_to_all | solution.py:342
  54.5 0.0 copy-done.2
  54.5 0.5 output_kernel.1
  55.0 13.2 %all_to_all.27 = f32[8,8,128]{2,1,0:T(8,128)S(1)} all-to-all(f32[8,8,128]{2,1,0:T(8,128)S(1)} %bitcast.23), channel_id=1, replica_groups=mesh['ctx'=128,'head'=8] {'head'}, dimensions={0} | all-to-all | bytes 65536 | tf_op jit(solution)/shard_map/all_to_all | solution.py:408
  68.3 1.0 grad_kernel.1
  69.2 0.0 copy-start
  69.2 0.0 copy-start.1
  69.2 0.0 copy-start.6
  69.2 7.6 %all-to-all-start.3 = ((f32[64,8,128]{2,1,0:T(8,128)}), f32[64,8,128]{2,1,0:T(8,128)S(1)}, u32[]{:S(2)}, u32[]{:S(2)}) async-start(f32[64,8,128]{2,1,0:T(8,128)} %bitcast.9), calls=%async_computation.3 | async-start | bytes 524288 | tf_op jit(solution)/shard_map/all_to_all | solution.py:342
  76.9 0.0 copy-start.5
  76.9 0.0 copy-start.7
  76.9 0.0 copy-done
  76.9 0.0 copy-done.1
  76.9 0.0 copy-done.6
  76.9 0.6 copy-done.5
  77.6 0.0 copy-done.7
  77.6 1.5 %intra_kernel.1 = (bf16[128,512]{1,0:T(8,128)(2,1)}, bf16[128,512]{1,0:T(8,128)(2,1)}) custom-call(s32[1]{0:T(128)} %bitcast.start_ref, bf16[128,512]{1,0:T(8,128)(2,1)S(1)} %copy-done.1, bf16[128,512]{1,0:T(8,128)(2,1)S(1)} %copy-done, f32[1,512]{1,0:T(1,128)S(1)} %bitcast.25, f32[4,128]{1,0:T(4,128)S(1)} %copy-done.5, s32[1,128]{1,0:T(1,128)S(1)} %bitcast.28, ...), custom_call_target="tpu_custom_call" | custom-call | tf_op jit(solution)/shard_map/intra_kernel/pallas_call | solution.py:328
  79.1 2.1 %part_kernel.1 = (f32[128,512]{1,0:T(8,128)S(1)}, f32[128,512]{1,0:T(8,128)S(1)}, f32[512,128]{1,0:T(8,128)S(1)}, f32[512,128]{1,0:T(8,128)S(1)}) custom-call(s32[1]{0:T(128)} %bitcast.start_ref, bf16[128,512]{1,0:T(8,128)(2,1)S(1)} %copy-done.2, bf16[128,512]{1,0:T(8,128)(2,1)S(1)} %copy-done, f32[4,128]{1,0:T(4,128)S(1)} %copy-done.5, ...), custom_call_target="tpu_custom_call" | custom-call | tf_op jit(solution)/shard_map/part_kernel/pallas_call | solution.py:328
  81.2 0.0 copy-start.3
  81.2 7.2 %all-to-all-done.3 = f32[64,8,128]{2,1,0:T(8,128)S(1)} async-done(((f32[64,8,128]{2,1,0:T(8,128)}), f32[64,8,128]{2,1,0:T(8,128)S(1)}, u32[]{:S(2)}, u32[]{:S(2)}) %all-to-all-start.3) | async-done | bytes 262176 | tf_op jit(solution)/shard_map/all_to_all | solution.py:342
  88.4 0.1 backward_kernel.1
  88.6 0.0 copy-done.3
  88.6 17.5 %all_to_all.28 = f32[64,8,128]{2,1,0:T(8,128)S(1)} all-to-all(f32[64,8,128]{2,1,0:T(8,128)S(1)} %bitcast.18), channel_id=1, replica_groups={{128,136,144,152,160,168,176,184,192,200,208,216,224,232,240,248,256,26..., dimensions={0} | all-to-all | bytes 524288 | tf_op jit(solution)/shard_map/all_to_all | solution.py:342
  106.1 0.0 copy-start.4
  106.1 0.8 collective-permute-start.1
  106.9 0.0 collective-permute-done.1.edge_ref
  106.9 0.1 copy-done.4
  107.0 1.0 final_kernel.1
  (3 shorter events, 0.1 us)
Async XLA Ops:
  0.7 3.1 %collective-permute-start = (f32[512,128]{1,0:T(8,128)S(1)}, f32[512,128]{1,0:T(8,128)S(1)}, u32[]{:S(2)}, u32[]{:S(2)}) collective-permute-start(f32[512,128]{1,0:T(8,128)S(1)} %source_kernel.1), channel_id=1, source_target_pairs={{504,512},{505,513},{506,514},{507,515},{508,516},{509,517},{510,5... | collective-permute-start | bytes 786440 | tf_op jit(solution)/shard_map/ppermute | solution.py:371
  36.9 17.6 %copy-start.2 = (bf16[128,512]{1,0:T(8,128)(2,1)S(1)}, bf16[128,512]{1,0:T(8,128)(2,1)}, u32[]{:S(2)}) copy-start(bf16[128,512]{1,0:T(8,128)(2,1)} %query_ref.5) | copy-start | bytes 393220
  69.2 7.7 %copy-start = (bf16[128,512]{1,0:T(8,128)(2,1)S(1)}, bf16[128,512]{1,0:T(8,128)(2,1)}, u32[]{:S(2)}) copy-start(bf16[128,512]{1,0:T(8,128)(2,1)} %value_ref.7) | copy-start | bytes 393220
  69.2 7.7 %copy-start.1 = (bf16[128,512]{1,0:T(8,128)(2,1)S(1)}, bf16[128,512]{1,0:T(8,128)(2,1)}, u32[]{:S(2)}) copy-start(bf16[128,512]{1,0:T(8,128)(2,1)} %key_ref.5) | copy-start | bytes 393220
  69.2 7.7 %copy-start.6 = (f32[512]{0:T(512)S(1)}, f32[512]{0:T(512)}, u32[]{:S(2)}) copy-start(f32[512]{0:T(512)} %param.13) | copy-start | bytes 6148
  69.2 19.2 %all-to-all-start.3 = ((f32[64,8,128]{2,1,0:T(8,128)}), f32[64,8,128]{2,1,0:T(8,128)S(1)}, u32[]{:S(2)}, u32[]{:S(2)}) async-start(f32[64,8,128]{2,1,0:T(8,128)} %bitcast.9), calls=%async_computation.3 | async-start | bytes 524288 | tf_op jit(solution)/shard_map/all_to_all | solution.py:342
  76.9 0.7 copy-start.5
  76.9 0.7 copy-start.7
  81.2 7.4 %copy-start.3 = (f32[512,128]{1,0:T(8,128)}, f32[512,128]{1,0:T(8,128)S(1)}, u32[]{:S(2)}) copy-start(f32[512,128]{1,0:T(8,128)S(1)} %get-tuple-element.54.outward_ref) | copy-start | bytes 786436
  106.1 1.0 copy-start.4
  106.1 0.8 collective-permute-start.1

commit v9 on v8

--- a/solution.py
+++ b/solution.py
@@ -14,7 +14,7 @@
 F32 = jnp.float32
 BF16 = jnp.bfloat16
 HIGH = lax.Precision.HIGHEST
-TURN = 16
+TURN = 32
 GROUPS = [[half * HALF + (p + TURN) % HALF for p in range(HALF)] for half in range(2)]
 
 

time: 110 us -> 109 us (level)
  no operation moved by 1% of the time
where the time goes in v9:
time: 109 us; the launch traced here: 108 us
  blocking collectives  80.9 us (74%)
  starting transfers between devices  9 us (8%)
  Pallas kernels  8.92 us (8%)
  waiting for transfers between devices  7.24 us (7%)
    all_to_all x3, blocking collectives, exchange(): lax.all_to_all(rows.reshape(shape), 'ctx', 0, 0, axis_index_groups=GROUPS...  67.7 us
    all_to_all x1, blocking collectives, on_device(): lax.all_to_all(sums.reshape(peers, SUB, DH), 'head', 0, 0, tiled=True)  13.2 us
    pallas_call x10, Pallas kernels, call(): pl.pallas_call(kernel, out_shape=tuple((pltpu.VMEM(shape, kind) if keep e...  8.87 us
    all_to_all x1, starting transfers between devices, exchange(): lax.all_to_all(rows.reshape(shape), 'ctx', 0, 0, axis_index_groups=GROUPS...  7.51 us
    all_to_all x1, waiting for transfers between devices, exchange(): lax.all_to_all(rows.reshape(shape), 'ctx', 0, 0, axis_index_groups=GROUPS...  7.23 us
  transfers between devices with their start and end apart: 3, of which 1 were waited for; matrix products, arithmetic and copies ran while one was open for 0% of the time, Pallas kernels for 6%

profile of v9, /device:TPU:1, one launch (start us, length us, event | category | flops | bytes accessed | tf_op | source)
XLA Modules:
  0.0 107.6 jit_solution(16716189989080986907)
XLA Ops:
  0.7 0.7 collective-permute-start
  1.4 2.4 %local_kernel.1 = (f32[512,128]{1,0:T(8,128)S(1)}, f32[4,128]{1,0:T(4,128)S(1)}, bf16[512,128]{1,0:T(8,128)(2,1)S(1)}, f32[128,512]{1,0:T(8,128)S(1)}, f32[512,128]{1,0:T(8,128)S(1)}, /*index=5*/f32[128,512]{1,0:T(8,128)S(1)}) custom-call(s32[1]{0:T(128)} %bitcast.start_ref, bf16[128,512]{1,0:T(8,128)(2,1)} %query_ref.5, bf16[128,512]{1,0:T(8,128)(2,1)} %key_ref.5, ...), custom_call_target="tpu_custom_call" | custom-call | tf_op jit(solution)/shard_map/local_kernel/pallas_call | solution.py:328
  3.8 0.0 collective-permute-done.edge_ref
  3.8 32.8 %all_to_all.25 = f32[64,9,1,128]{3,2,1,0:T(1,128)S(1)} all-to-all(f32[64,9,1,128]{3,2,1,0:T(1,128)S(1)} %bitcast.15), channel_id=1, replica_groups={{256,264,272,280,288,296,304,312,320,328,336,344,352,360,368,376,384,39..., dimensions={0} | all-to-all | bytes 589824 | tf_op jit(solution)/shard_map/all_to_all | solution.py:342
  36.6 0.1 forward_kernel.1
  36.8 0.0 copy-start.2
  36.8 17.5 %all_to_all.26 = f32[64,8,128]{2,1,0:T(8,128)S(1)} all-to-all(f32[64,8,128]{2,1,0:T(8,128)S(1)} %bitcast.22), channel_id=1, replica_groups={{256,264,272,280,288,296,304,312,320,328,336,344,352,360,368,376,384,39..., dimensions={0} | all-to-all | bytes 524288 | tf_op jit(solution)/shard_map/all_to_all | solution.py:342
  54.3 0.0 copy-done.2
  54.3 0.5 output_kernel.1
  54.8 13.2 %all_to_all.27 = f32[8,8,128]{2,1,0:T(8,128)S(1)} all-to-all(f32[8,8,128]{2,1,0:T(8,128)S(1)} %bitcast.23), channel_id=1, replica_groups=mesh['ctx'=128,'head'=8] {'head'}, dimensions={0} | all-to-all | bytes 65536 | tf_op jit(solution)/shard_map/all_to_all | solution.py:408
  68.0 1.0 grad_kernel.1
  69.0 0.0 copy-start
  69.0 0.0 copy-start.1
  69.0 0.0 copy-start.6
  69.0 7.5 %all-to-all-start.3 = ((f32[64,8,128]{2,1,0:T(8,128)}), f32[64,8,128]{2,1,0:T(8,128)S(1)}, u32[]{:S(2)}, u32[]{:S(2)}) async-start(f32[64,8,128]{2,1,0:T(8,128)} %bitcast.9), calls=%async_computation.3 | async-start | bytes 524288 | tf_op jit(solution)/shard_map/all_to_all | solution.py:342
  76.6 0.0 copy-start.5
  76.6 0.0 copy-start.7
  76.6 0.0 copy-done
  76.6 0.0 copy-done.1
  76.6 0.0 copy-done.6
  76.6 0.6 copy-done.5
  77.2 0.0 copy-done.7
  77.2 1.5 %intra_kernel.1 = (bf16[128,512]{1,0:T(8,128)(2,1)}, bf16[128,512]{1,0:T(8,128)(2,1)}) custom-call(s32[1]{0:T(128)} %bitcast.start_ref, bf16[128,512]{1,0:T(8,128)(2,1)S(1)} %copy-done.1, bf16[128,512]{1,0:T(8,128)(2,1)S(1)} %copy-done, f32[1,512]{1,0:T(1,128)S(1)} %bitcast.25, f32[4,128]{1,0:T(4,128)S(1)} %copy-done.5, s32[1,128]{1,0:T(1,128)S(1)} %bitcast.28, ...), custom_call_target="tpu_custom_call" | custom-call | tf_op jit(solution)/shard_map/intra_kernel/pallas_call | solution.py:328
  78.8 2.1 %part_kernel.1 = (f32[128,512]{1,0:T(8,128)S(1)}, f32[128,512]{1,0:T(8,128)S(1)}, f32[512,128]{1,0:T(8,128)S(1)}, f32[512,128]{1,0:T(8,128)S(1)}) custom-call(s32[1]{0:T(128)} %bitcast.start_ref, bf16[128,512]{1,0:T(8,128)(2,1)S(1)} %copy-done.2, bf16[128,512]{1,0:T(8,128)(2,1)S(1)} %copy-done, f32[4,128]{1,0:T(4,128)S(1)} %copy-done.5, ...), custom_call_target="tpu_custom_call" | custom-call | tf_op jit(solution)/shard_map/part_kernel/pallas_call | solution.py:328
  80.9 0.0 copy-start.3
  80.9 7.2 %all-to-all-done.3 = f32[64,8,128]{2,1,0:T(8,128)S(1)} async-done(((f32[64,8,128]{2,1,0:T(8,128)}), f32[64,8,128]{2,1,0:T(8,128)S(1)}, u32[]{:S(2)}, u32[]{:S(2)}) %all-to-all-start.3) | async-done | bytes 262176 | tf_op jit(solution)/shard_map/all_to_all | solution.py:342
  88.1 0.1 backward_kernel.1
  88.2 0.0 copy-done.3
  88.2 17.4 %all_to_all.28 = f32[64,8,128]{2,1,0:T(8,128)S(1)} all-to-all(f32[64,8,128]{2,1,0:T(8,128)S(1)} %bitcast.18), channel_id=1, replica_groups={{256,264,272,280,288,296,304,312,320,328,336,344,352,360,368,376,384,39..., dimensions={0} | all-to-all | bytes 524288 | tf_op jit(solution)/shard_map/all_to_all | solution.py:342
  105.6 0.0 copy-start.4
  105.6 0.8 collective-permute-start.1
  106.5 0.0 collective-permute-done.1.edge_ref
  106.5 0.1 copy-done.4
  106.6 1.0 final_kernel.1
  (3 shorter events, 0.1 us)
Async XLA Ops:
  0.7 3.1 %collective-permute-start = (f32[512,128]{1,0:T(8,128)S(1)}, f32[512,128]{1,0:T(8,128)S(1)}, u32[]{:S(2)}, u32[]{:S(2)}) collective-permute-start(f32[512,128]{1,0:T(8,128)S(1)} %source_kernel.1), channel_id=1, source_target_pairs={{504,512},{505,513},{506,514},{507,515},{508,516},{509,517},{510,5... | collective-permute-start | bytes 786440 | tf_op jit(solution)/shard_map/ppermute | solution.py:371
  36.8 17.5 %copy-start.2 = (bf16[128,512]{1,0:T(8,128)(2,1)S(1)}, bf16[128,512]{1,0:T(8,128)(2,1)}, u32[]{:S(2)}) copy-start(bf16[128,512]{1,0:T(8,128)(2,1)} %query_ref.5) | copy-start | bytes 393220
  69.0 7.6 %copy-start = (bf16[128,512]{1,0:T(8,128)(2,1)S(1)}, bf16[128,512]{1,0:T(8,128)(2,1)}, u32[]{:S(2)}) copy-start(bf16[128,512]{1,0:T(8,128)(2,1)} %value_ref.7) | copy-start | bytes 393220
  69.0 7.6 %copy-start.1 = (bf16[128,512]{1,0:T(8,128)(2,1)S(1)}, bf16[128,512]{1,0:T(8,128)(2,1)}, u32[]{:S(2)}) copy-start(bf16[128,512]{1,0:T(8,128)(2,1)} %key_ref.5) | copy-start | bytes 393220
  69.0 7.6 %copy-start.6 = (f32[512]{0:T(512)S(1)}, f32[512]{0:T(512)}, u32[]{:S(2)}) copy-start(f32[512]{0:T(512)} %param.13) | copy-start | bytes 6148
  69.0 19.1 %all-to-all-start.3 = ((f32[64,8,128]{2,1,0:T(8,128)}), f32[64,8,128]{2,1,0:T(8,128)S(1)}, u32[]{:S(2)}, u32[]{:S(2)}) async-start(f32[64,8,128]{2,1,0:T(8,128)} %bitcast.9), calls=%async_computation.3 | async-start | bytes 524288 | tf_op jit(solution)/shard_map/all_to_all | solution.py:342
  76.6 0.7 copy-start.5
  76.6 0.7 copy-start.7
  80.9 7.4 %copy-start.3 = (f32[512,128]{1,0:T(8,128)}, f32[512,128]{1,0:T(8,128)S(1)}, u32[]{:S(2)}) copy-start(f32[512,128]{1,0:T(8,128)S(1)} %get-tuple-element.54.outward_ref) | copy-start | bytes 786436
  105.6 1.0 copy-start.4
  105.6 0.8 collective-permute-start.1
